TPU v7x, 32 devices: a whole 2x2x4 slice. The times are simulated.
32 devices in a mesh: grp: 2 (over x), seq: 4 (over y, core), sub: 4 (over z).
Axes of the slice: x: 2, y: 2, z: 4, core: 2. Of those that a mesh axis runs over, the one named last changes fastest.
Arguments:
- query_rows: bfloat16 [8, 512, 2048], P(('grp', 'sub'), 'seq'), parts along dimension 0, may hold values from -9 to 9
- key_rows: bfloat16 [8, 512, 256], P(('grp', 'sub'), 'seq'), parts along dimension 0, may hold values from -4 to 4
- value_rows: bfloat16 [8, 512, 256], P(('grp', 'sub'), 'seq'), parts along dimension 0, may hold values from -6 to 6
- residual_in: bfloat16 [8, 512, 2048], P(('grp', 'sub'), 'seq'), parts along dimension 0, may hold values from -6 to 6
- out_proj: bfloat16 [2048, 2048], P('seq'), may hold values from -0.5 to 0.5
- norm_gain: bfloat16 [2048], replicated, may hold values from 0.099609375 to 1.8984375
- expert_ids: int32 [8, 512, 8], P(('grp', 'sub'), 'seq'), parts along dimension 0, may hold values from 0 to 15, all different within a row; in each aligned block of 128 rows (0 to 127, 128 to 255, ..., all dimensions but the last counted through in order) at most 80 rows name the same one
- gate_weights: bfloat16 [8, 512, 8], P(('grp', 'sub'), 'seq'), parts along dimension 0, may hold values from 0.049804688 to 1
- expert_gate: bfloat16 [16, 2048, 768], P(('seq', 'sub')), may hold values from -0.125 to 0.125
- expert_up: bfloat16 [16, 2048, 768], P(('seq', 'sub')), may hold values from -0.125 to 0.125
- expert_down: bfloat16 [16, 768, 2048], P(('seq', 'sub')), may hold values from -0.21875 to 0.21875
Outputs:
- layer_out: bfloat16 [8, 512, 2048], P(('grp', 'sub'), 'seq'), parts along dimension 0
There are 2 independent parts, one for each index of `grp`. A program takes and returns all parts, laid end to end along the dimension named above; an argument that names none is the same for every part. Nothing has to cross between parts.
Inputs may be any that keep to these rules, and one draw needn't show every extreme that they name: `expert_ids`: A row names 8 different experts. In each aligned block of 128 rows (the rows of one device) no expert is named by more than 80 rows, a bound that some block reaches.
All inputs are finite; a program needn't handle non-finite values.
Results may differ from a plain program's by a relative error of at most 0.013.
Values may be sent and summed in bfloat16 or wider, within the bound.
A program may use at most 128 MiB of HBM per device.

v0:
```python
import functools
import jax
import jax.numpy as jnp
from jax import lax
from jax.experimental import pallas as pl
from jax.experimental.pallas import tpu as pltpu
from jax.sharding import PartitionSpec as P

D = 2048
HD = 128
QH = 16
KVH = 2


def attend_head(queries, keys_one, values_one, block):
    length = queries.shape[0]
    scale = 1.0 / queries.shape[1] ** 0.5
    pieces = []
    for part_index in range(length // block):
        stop = (part_index + 1) * block
        rows_here = queries[part_index * block : stop]
        scores = (
            jnp.einsum("qd,kd->qk", rows_here, keys_one[:stop], preferred_element_type=jnp.float32)
            * scale
        )
        row_pos = part_index * block + jnp.arange(block, dtype=jnp.int32)
        col_pos = jnp.arange(stop, dtype=jnp.int32)
        scores = jnp.where(row_pos[:, None] >= col_pos[None, :], scores, -1e30)
        peak = jnp.max(scores, axis=1, keepdims=True)
        weights = jnp.exp(scores - peak)
        probs = (weights / jnp.sum(weights, axis=1, keepdims=True)).astype(jnp.bfloat16)
        pieces.append(
            jnp.dot(probs, values_one[:stop], preferred_element_type=jnp.float32).astype(
                jnp.bfloat16
            )
        )
    return jnp.concatenate(pieces, axis=0)


def rank_in_expert(flat_ids, experts):
    items = flat_ids.shape[0]
    width = 128
    n_parts = items // width
    onehot = (
        (flat_ids[:, None] == jnp.arange(experts, dtype=jnp.int32)[None, :])
        .astype(jnp.bfloat16)
        .reshape(n_parts, width, experts)
    )
    lower = (
        jnp.arange(width, dtype=jnp.int32)[:, None] > jnp.arange(width, dtype=jnp.int32)[None, :]
    ).astype(jnp.bfloat16)
    within = jnp.einsum("ij,bje->bie", lower, onehot, preferred_element_type=jnp.float32)
    part_counts = jnp.sum(onehot.astype(jnp.float32), axis=1)
    earlier = jnp.cumsum(part_counts, axis=0) - part_counts
    ranks = jnp.sum((within + earlier[:, None, :]) * onehot.astype(jnp.float32), axis=2)
    return ranks.reshape(items).astype(jnp.int32)


def per_device_routed(
    query_rows,
    key_rows,
    value_rows,
    residual_in,
    out_proj,
    norm_gain,
    expert_ids,
    gate_weights,
    expert_gate,
    expert_up,
    expert_down,
):
    tokens = query_rows.shape[1]
    n_seq = lax.axis_size("seq")
    n_sub = lax.axis_size("sub")
    heads_here = QH // n_seq
    group = QH // KVH
    query_local = lax.all_to_all(query_rows, "seq", split_axis=2, concat_axis=1, tiled=True)
    key_full, value_full = (
        lax.all_gather(key_rows, "seq", axis=1, tiled=True),
        lax.all_gather(value_rows, "seq", axis=1, tiled=True),
    )
    first_head = lax.axis_index("seq") * heads_here
    key_list = []
    value_list = []
    for head in range(heads_here):
        kv_start = (first_head + head) // group * HD
        key_list.append(lax.dynamic_slice_in_dim(key_full[0], kv_start, HD, 1))
        value_list.append(lax.dynamic_slice_in_dim(value_full[0], kv_start, HD, 1))
    length = query_local.shape[1]
    block = min(length, max(512, length // 8))
    outputs = [
        attend_head(
            query_local[0, :, head * HD : (head + 1) * HD], key_list[head], value_list[head], block
        )
        for head in range(heads_here)
    ]
    head_block = jnp.concatenate(outputs, axis=1)[None]
    attended = lax.all_to_all(head_block, "seq", split_axis=1, concat_axis=2, tiled=True)[0]
    projected = jnp.dot(
        attended,
        lax.all_gather(out_proj, "seq", axis=0, tiled=True),
        preferred_element_type=jnp.float32,
    )
    hidden = (residual_in[0].astype(jnp.float32) + projected).astype(jnp.bfloat16)
    wide = hidden.astype(jnp.float32)
    normed = (
        wide
        * lax.rsqrt(jnp.mean(wide * wide, axis=1, keepdims=True) + 1e-06)
        * norm_gain.astype(jnp.float32)
    ).astype(jnp.bfloat16)
    topk = expert_ids.shape[2]
    experts = n_seq * n_sub
    cap = max(2, (5 * tokens * topk + 4 * experts - 1) // (4 * experts))
    flat_ids = expert_ids[0].reshape(-1)
    items = flat_ids.shape[0]
    ranks = rank_in_expert(flat_ids, experts)
    slot_of = flat_ids * cap + ranks
    slots_out = experts * cap
    item_of_slot = (
        jnp.full((slots_out,), items, jnp.int32).at[slot_of].set(jnp.arange(items, dtype=jnp.int32))
    )
    padded_rows = jnp.concatenate([normed, jnp.zeros((1, D), jnp.bfloat16)], axis=0)
    padded_gates = jnp.concatenate(
        [gate_weights[0].reshape(-1), jnp.zeros((1,), jnp.bfloat16)], axis=0
    )
    token_of_slot = jnp.where(item_of_slot < items, item_of_slot // topk, tokens)
    send_rows = padded_rows[token_of_slot].reshape(experts, cap, D)
    send_gates = padded_gates[item_of_slot].reshape(experts, cap)
    recv_rows, recv_gates = (
        lax.all_to_all(send_rows, ("seq", "sub"), split_axis=0, concat_axis=0, tiled=True),
        lax.all_to_all(send_gates, ("seq", "sub"), split_axis=0, concat_axis=0, tiled=True),
    )
    slots_in = experts * cap
    valid = recv_gates > 0
    counts = jnp.sum(valid.astype(jnp.int32), axis=1)
    offsets = jnp.cumsum(counts) - counts
    dest = jnp.where(
        valid, offsets[:, None] + jnp.arange(cap, dtype=jnp.int32)[None, :], slots_in
    ).reshape(-1)
    source_of = (
        jnp.full((slots_in + 1,), slots_in, jnp.int32)
        .at[dest]
        .set(jnp.arange(slots_in, dtype=jnp.int32))[:slots_in]
    )
    compact_rows = jnp.concatenate(
        [recv_rows.reshape(slots_in, D), jnp.zeros((1, D), jnp.bfloat16)], axis=0
    )[source_of]
    compact_gates = jnp.concatenate(
        [recv_gates.reshape(-1), jnp.zeros((1,), jnp.bfloat16)], axis=0
    )[source_of].astype(jnp.float32)
    filled = jnp.sum(counts)
    n_blocks = (filled + slots_in - 1) // slots_in
    w_gate = expert_gate[0]
    w_up = expert_up[0]
    w_down = expert_down[0]

    def expert_block(index, results):
        gate_proj = jnp.dot(compact_rows, w_gate, preferred_element_type=jnp.float32)
        up_proj = jnp.dot(compact_rows, w_up, preferred_element_type=jnp.float32)
        inner = (jax.nn.silu(gate_proj) * up_proj).astype(jnp.bfloat16)
        weighted = (
            jnp.dot(inner, w_down, preferred_element_type=jnp.float32) * compact_gates[:, None]
        )
        return weighted.astype(jnp.bfloat16)

    results = lax.fori_loop(0, n_blocks, expert_block, jnp.zeros((slots_in, D), jnp.bfloat16))
    returned = jnp.concatenate([results, jnp.zeros((1, D), jnp.bfloat16)], axis=0)[dest].reshape(
        experts, cap, D
    )
    back = lax.all_to_all(
        returned, ("seq", "sub"), split_axis=0, concat_axis=0, tiled=True
    ).reshape(slots_out, D)
    gathered = back[slot_of].reshape(tokens, topk, D).astype(jnp.float32)
    mixture = jnp.sum(gathered, axis=1)
    return (wide + mixture).astype(jnp.bfloat16)[None]


def nearest_order(n):
    return [sorted(range(n), key=lambda p: (abs(p - z), p)) for z in range(n)]


def lookup(table, i, j):
    total = 0
    for a, row in enumerate(table):
        for b, value in enumerate(row):
            if value:
                hit = jnp.logical_and(i == a, j == b)
                total = total + jnp.where(hit, value, 0)
    return total


def layer_kernel(
    n_sub,
    q_hbm,
    k_hbm,
    v_hbm,
    residual_ref,
    proj_hbm,
    gain_ref,
    coeff_ref,
    wg_hbm,
    wu_hbm,
    wd_hbm,
    o_ref,
    q_all,
    k_all,
    v_all,
    proj,
    partial,
    core_far,
    core_near,
    across_near,
    wide_ref,
    q_send,
    q_recv,
    kv_send,
    kv_recv,
    part_send,
    part_recv,
    rows,
    outs,
    from_core,
    from_y,
    from_low,
    from_high,
    from_mate,
    wg,
    wu,
    wd,
    load_sem,
    row_recv,
    up_send,
    down_send,
    y_send,
    core_send,
    relay_send,
    core_recv,
    result_send,
    y_recv,
    result_y_send,
    low_recv,
    high_recv,
    result_up_send,
    result_down_send,
    mate_send,
    mate_recv,
):
    seq = lax.axis_index("seq")
    z = lax.axis_index("sub")
    y = seq // 2
    c = seq % 2
    tokens = residual_ref.shape[0]
    width = residual_ref.shape[1]
    share = q_all.shape[1]
    heads = share // HD
    length = q_all.shape[0]
    group = QH // KVH
    half = tokens // 2
    order = nearest_order(n_sub)
    me = seq * n_sub + z
    high = {"sub": z + 1}
    low = {"sub": z - 1}
    across = {"seq": (1 - y) * 2 + c}
    partner = {"seq": y * 2 + 1 - c}
    diagonal = {"seq": (1 - y) * 2 + 1 - c}
    mate = z + 1 - 2 * (z % 2)
    beside = {"sub": mate}
    has_high = z < n_sub - 1
    has_low = z > 0

    def slot(yy, p, cc):
        return (yy * n_sub + p) * 2 + cc

    def piece(ref, index, h):
        return ref.at[pl.ds(pl.multiple_of(index * tokens + h * half, half), half), :]

    def remote(src, dst, send, recv, target):
        return pltpu.make_async_remote_copy(
            src_ref=src,
            dst_ref=dst,
            send_sem=send,
            recv_sem=recv,
            device_id=target,
            device_id_type=pl.DeviceIdType.MESH,
        )

    def query_part(s):
        return q_hbm.at[:, pl.ds(pl.multiple_of(s * share, share), share)]

    def cache_part(ref, s):
        return ref.at[:, pl.ds(pl.multiple_of(s * heads // group * HD, HD), HD)]

    def token_rows(ref, s):
        return ref.at[pl.ds(pl.multiple_of(s * tokens, tokens), tokens), :]

    own_parts = [
        pltpu.make_async_copy(query_part(seq), token_rows(q_all, seq), load_sem.at[0]),
        pltpu.make_async_copy(cache_part(k_hbm, seq), token_rows(k_all, seq), load_sem.at[1]),
        pltpu.make_async_copy(cache_part(v_hbm, seq), token_rows(v_all, seq), load_sem.at[2]),
        pltpu.make_async_copy(proj_hbm, proj, load_sem.at[3]),
    ]
    loads = [
        pltpu.make_async_copy(wg_hbm, wg, load_sem.at[4]),
        pltpu.make_async_copy(wu_hbm, wu, load_sem.at[5]),
        pltpu.make_async_copy(wd_hbm, wd, load_sem.at[6]),
    ]
    for load in own_parts + loads:
        load.start()

    barrier = pltpu.get_barrier_semaphore()
    pl.semaphore_signal(barrier, 1, device_id=across, device_id_type=pl.DeviceIdType.MESH)
    pl.semaphore_signal(barrier, 1, device_id=partner, device_id_type=pl.DeviceIdType.MESH)

    pl.semaphore_signal(barrier, 1, device_id=diagonal, device_id_type=pl.DeviceIdType.MESH)

    @pl.when(has_high)
    def _():
        pl.semaphore_signal(barrier, 1, device_id=high, device_id_type=pl.DeviceIdType.MESH)

    @pl.when(has_low)
    def _():
        pl.semaphore_signal(barrier, 1, device_id=low, device_id_type=pl.DeviceIdType.MESH)

    peers = 3 + jnp.where(has_high, 1, 0) + jnp.where(has_low, 1, 0)
    pl.semaphore_wait(barrier, peers)

    others = (
        ((1 - y) * 2 + c, across),
        ((1 - y) * 2 + 1 - c, diagonal),
        (y * 2 + 1 - c, partner),
    )

    def scatter_copies(s, target):
        return (
            remote(
                cache_part(k_hbm, s),
                token_rows(k_all, seq),
                kv_send.at[s],
                kv_recv.at[seq],
                target,
            ),
            remote(
                cache_part(v_hbm, s),
                token_rows(v_all, seq),
                kv_send.at[4 + s],
                kv_recv.at[4 + seq],
                target,
            ),
            remote(
                query_part(s), token_rows(q_all, seq), q_send.at[s], q_recv.at[seq], target
            ),
        )

    for s, target in others:
        for copy in scatter_copies(s, target):
            copy.start()

    def arrival(ref, s, sem):
        return remote(token_rows(ref, s), token_rows(ref, s), q_send.at[s], sem, partner)

    for load in own_parts:
        load.wait()
    for s, _ in others:
        arrival(k_all, s, kv_recv.at[s]).wait_recv()
        arrival(v_all, s, kv_recv.at[4 + s]).wait_recv()
        arrival(q_all, s, q_recv.at[s]).wait_recv()

    far_copy = remote(
        token_rows(partial, (1 - y) * 2 + 1 - c), core_far, part_send.at[0], part_recv.at[0], partner
    )
    across_copy = remote(
        token_rows(partial, (1 - y) * 2 + c),
        across_near,
        part_send.at[1],
        part_recv.at[1],
        across,
    )
    near_copy = remote(
        token_rows(partial, y * 2 + 1 - c), core_near, part_send.at[2], part_recv.at[2], partner
    )

    def attend_step(j, carry):
        yy = jnp.where(j < 2, 1 - y, y)
        cc = jnp.where(j % 2 == 0, 1 - c, c)
        i = yy * 2 + cc
        at = pl.ds(pl.multiple_of(i * tokens, tokens), tokens)
        row_pos = i * tokens + lax.broadcasted_iota(jnp.int32, (tokens, length), 0)
        col_pos = lax.broadcasted_iota(jnp.int32, (tokens, length), 1)
        allowed = row_pos >= col_pos
        outputs = []
        for head in range(heads):
            scores = lax.dot_general(
                q_all[at, head * HD : (head + 1) * HD],
                k_all[...],
                (((1,), (1,)), ((), ())),
                preferred_element_type=jnp.float32,
            ) * (1.0 / HD**0.5)
            scores = jnp.where(allowed, scores, -1e30)
            weights = jnp.exp(scores - jnp.max(scores, axis=1, keepdims=True))
            total = jnp.sum(weights, axis=1, keepdims=True)
            probs = (weights * (1.0 / total)).astype(jnp.bfloat16)
            outputs.append(
                jnp.dot(probs, v_all[...], preferred_element_type=jnp.float32).astype(jnp.bfloat16)
            )
        projected = jnp.dot(
            jnp.concatenate(outputs, axis=1), proj[...], preferred_element_type=jnp.float32
        )

        @pl.when(j != 1)
        def _():
            partial[at, :] = projected.astype(jnp.bfloat16)

        @pl.when(j == 0)
        def _():
            far_copy.start()

        @pl.when(j == 1)
        def _():
            far_copy.wait_recv()
            partial[at, :] = (projected + core_far[...].astype(jnp.float32)).astype(jnp.bfloat16)
            across_copy.start()

        @pl.when(j == 2)
        def _():
            near_copy.start()

        return carry

    lax.fori_loop(0, 4, attend_step, 0)
    near_copy.wait_recv()
    own_rows = pl.ds(pl.multiple_of(seq * tokens, tokens), tokens)
    base = (
        residual_ref[...].astype(jnp.float32)
        + partial[own_rows, :].astype(jnp.float32)
        + core_near[...].astype(jnp.float32)
    )
    across_copy.wait_recv()
    hidden = (base + across_near[...].astype(jnp.float32)).astype(jnp.bfloat16)
    wide_ref[...] = hidden
    wide = hidden.astype(jnp.float32)
    normed = (
        wide
        * lax.rsqrt(jnp.mean(wide * wide, axis=1, keepdims=True) + 1e-06)
        * gain_ref[...].astype(jnp.float32)
    ).astype(jnp.bfloat16)
    own_slot = pl.ds(pl.multiple_of(slot(y, z, c) * tokens, tokens), tokens)
    rows[own_slot, :width] = normed
    rows[own_slot, width:] = coeff_ref[...]

    def row_copy(index, h, send, target):
        here = piece(rows, index, h)
        return remote(here, here, send, row_recv.at[index * 2 + h], target)

    def wait_rows(index, h):
        row_copy(index, h, relay_send.at[0], partner).wait_recv()

    def column_copies(p, h):
        index = slot(y, p, c)
        at = p * 2 + h
        return (
            (jnp.logical_and(p <= z, has_high), row_copy(index, h, up_send.at[at], high)),
            (jnp.logical_and(p >= z, has_low), row_copy(index, h, down_send.at[at], low)),
            (
                jnp.logical_or(p != mate, h == 0),
                row_copy(index, h, y_send.at[at], across),
            ),
            (None, row_copy(index, h, core_send.at[at], partner)),
        )

    def spread(p, h):
        for condition, copy in column_copies(p, h):
            if condition is None:
                copy.start()
            else:

                @pl.when(condition)
                def _():
                    copy.start()

    def relay_copy(p, h):
        return row_copy(slot(1 - y, p, c), h, relay_send.at[p * 2 + h], partner)

    def result_copy(yy, p):
        index = slot(yy, p, 1 - c)
        pair = yy * n_sub + p
        src = outs.at[pl.ds(pl.multiple_of(index * tokens, tokens), tokens), :]
        dst = from_core.at[pl.ds(pl.multiple_of(pair * tokens, tokens), tokens), :]
        return remote(src, dst, result_send.at[pair], core_recv.at[pair], partner)

    def compute(yy, p):
        wait_rows(slot(yy, p, 1 - c), 0)
        wait_rows(slot(yy, p, 1 - c), 1)
        at = pl.ds(pl.multiple_of((yy * n_sub + p) * 2 * tokens, 2 * tokens), 2 * tokens)
        x = rows[at, :width]
        gains = rows[at, width:].astype(jnp.float32)
        lane = lax.broadcasted_iota(jnp.int32, gains.shape, 1)
        coeff = jnp.sum(jnp.where(lane == me, gains, 0.0), axis=1, keepdims=True)
        gate = jnp.dot(x, wg[...], preferred_element_type=jnp.float32)
        up = jnp.dot(x, wu[...], preferred_element_type=jnp.float32)
        inner = (gate / (1.0 + jnp.exp(-gate)) * up).astype(jnp.bfloat16)
        out = jnp.dot(inner, wd[...], preferred_element_type=jnp.float32)
        outs[at, :] = (out * coeff).astype(jnp.bfloat16)
        result_copy(yy, p).start()

    for load in loads:
        load.wait()

    def mate_rows():
        return row_copy(slot(1 - y, z, c), 1, mate_send.at[0], beside)

    def gather_step(k, carry):
        t = (k + 1) // 2
        other = k % 2
        last = k == 2 * n_sub

        @pl.when(jnp.logical_or(k == 0, jnp.logical_and(other == 1, t < n_sub)))
        def _():
            p = lookup(order, z, t)

            @pl.when(t > 0)
            def _():
                wait_rows(slot(y, p, c), 0)

            spread(p, 0)

            @pl.when(t > 0)
            def _():
                wait_rows(slot(y, p, c), 1)

            spread(p, 1)

        @pl.when(k == 2 * n_sub - 3)
        def _():
            mate_rows().start()

        q = lookup(order, z, t - 1)

        @pl.when(other == 1)
        def _():
            wait_rows(slot(1 - y, q, c), 0)
            relay_copy(q, 0).start()

            @pl.when(q != mate)
            def _():
                wait_rows(slot(1 - y, q, c), 1)
                relay_copy(q, 1).start()

        @pl.when(last)
        def _():
            wait_rows(slot(1 - y, mate, c), 1)
            relay_copy(mate, 1).start()

        @pl.when(jnp.logical_or(other == 0, q != mate))
        def _():
            yy = jnp.where(jnp.logical_or(other == 1, last), 1 - y, y)
            p = jnp.where(last, mate, jnp.where(other == 1, q, lookup(order, z, t)))
            compute(yy, p)

        return carry

    lax.fori_loop(0, 2 * n_sub + 1, gather_step, 0)

    def wide_load(ref, index, h):
        at = pl.ds(pl.multiple_of(index * tokens + h * half, half), half)
        return ref[at, :].astype(jnp.float32)

    def y_copy(p, h):
        at = p * 2 + h
        return remote(
            piece(outs, slot(1 - y, p, c), h),
            piece(from_y, p, h),
            result_y_send.at[at],
            y_recv.at[at],
            across,
        )

    def z_copy(p, h, buffer, send, recv, target):
        at = p * 2 + h
        return remote(
            piece(outs, slot(y, p, c), h), piece(buffer, p, h), send.at[at], recv.at[at], target
        )

    def up_copy(p, h):
        return z_copy(p, h, from_low, result_up_send, low_recv, high)

    def down_copy(p, h):
        return z_copy(p, h, from_high, result_down_send, high_recv, low)

    def store_out(index, h, value):
        at = pl.ds(pl.multiple_of(index * tokens + h * half, half), half)
        outs[at, :] = value.astype(jnp.bfloat16)

    def mate_result(p):
        return remote(
            piece(outs, slot(1 - y, p, c), 1), from_mate, mate_send.at[1], mate_recv.at[0], beside
        )

    def y_step(k, carry):
        p = lookup(order, z, n_sub - 1 - k)
        result_copy(1 - y, p).wait_recv()
        index = slot(1 - y, p, c)
        for h in range(2):
            store_out(
                index, h, wide_load(outs, index, h) + wide_load(from_core, (1 - y) * n_sub + p, h)
            )

            @pl.when(jnp.logical_and(p == mate, h == 1))
            def _():
                mate_result(mate).start()

            @pl.when(jnp.logical_or(p != z, h == 0) & jnp.logical_or(p != mate, h == 0))
            def _():
                y_copy(p, h).start()

        return carry

    lax.fori_loop(0, n_sub, y_step, 0)

    def own_step(k, carry):
        p = lookup(order, z, n_sub - 1 - k)
        result_copy(y, p).wait_recv()
        index = slot(y, p, c)
        store = wide_load(outs, index, 0) + wide_load(from_core, y * n_sub + p, 0)
        store_out(index, 0, store)
        store = wide_load(outs, index, 1) + wide_load(from_core, y * n_sub + p, 1)
        store_out(index, 1, store)
        return carry

    lax.fori_loop(0, n_sub, own_step, 0)
    mate_result(z).wait_recv()
    store_out(
        slot(1 - y, z, c),
        1,
        wide_load(outs, slot(1 - y, z, c), 1) + from_mate[...].astype(jnp.float32),
    )
    y_copy(z, 1).start()

    def z_step(k, carry):
        p = lookup(order, z, n_sub - 1 - k // 2)
        h = k % 2
        index = slot(y, p, c)
        direct = jnp.logical_or(p != mate, h == 0)

        @pl.when(direct)
        def _():
            y_copy(p, h).wait_recv()
            store_out(index, h, wide_load(outs, index, h) + wide_load(from_y, p, h))

        @pl.when(p > z)
        def _():
            @pl.when(has_low)
            def _():
                up_copy(p, h).wait_recv()
                store_out(index, h, wide_load(outs, index, h) + wide_load(from_low, p, h))

            up_copy(p, h).start()

        @pl.when(p < z)
        def _():
            @pl.when(has_high)
            def _():
                down_copy(p, h).wait_recv()
                store_out(index, h, wide_load(outs, index, h) + wide_load(from_high, p, h))

            down_copy(p, h).start()

        @pl.when(p == z)
        def _():
            at = pl.ds(pl.multiple_of(h * half, half), half)
            @pl.when(has_low)
            def _():
                up_copy(p, h).wait_recv()
                store_out(index, h, wide_load(outs, index, h) + wide_load(from_low, p, h))

            @pl.when(has_high)
            def _():
                down_copy(p, h).wait_recv()
                store_out(index, h, wide_load(outs, index, h) + wide_load(from_high, p, h))

            o_ref[at, :] = (wide_ref[at, :].astype(jnp.float32) + wide_load(outs, index, h)).astype(
                jnp.bfloat16
            )

        return carry

    lax.fori_loop(0, 2 * n_sub, z_step, 0)

    def drain(k, carry):
        p = k // 2
        h = k % 2
        for condition, copy in column_copies(p, h):
            if condition is None:
                copy.wait_send()
            else:

                @pl.when(condition)
                def _():
                    copy.wait_send()

        relay_copy(p, h).wait_send()

        @pl.when(jnp.logical_or(p != mate, h == 0))
        def _():
            y_copy(p, h).wait_send()

        result_copy(h, p).wait_send()

        @pl.when(p > z)
        def _():
            up_copy(p, h).wait_send()

        @pl.when(p < z)
        def _():
            down_copy(p, h).wait_send()

        return carry

    lax.fori_loop(0, 2 * n_sub, drain, 0)
    for s, target in others:
        for copy in scatter_copies(s, target):
            copy.wait_send()
    mate_rows().wait_send()
    mate_result(mate).wait_send()
    far_copy.wait_send()
    across_copy.wait_send()
    near_copy.wait_send()


def layer(queries, keys, values, residual, proj, gain, coeffs, w_gate, w_up, w_down, n_sub):
    tokens, width = residual.shape
    share = proj.shape[0]
    blocks = 4 * n_sub
    dma = lambda count: pltpu.SemaphoreType.DMA((count,))
    hbm = pl.BlockSpec(memory_space=pl.ANY)
    vmem = pl.BlockSpec(memory_space=pltpu.VMEM)
    bf = jnp.bfloat16
    return pl.pallas_call(
        functools.partial(layer_kernel, n_sub),
        in_specs=[hbm, hbm, hbm, vmem, hbm, vmem, vmem, hbm, hbm, hbm],
        out_specs=vmem,
        out_shape=jax.ShapeDtypeStruct((tokens, width), bf),
        scratch_shapes=[
            pltpu.VMEM((4 * tokens, share), bf),
            pltpu.VMEM((4 * tokens, HD), bf),
            pltpu.VMEM((4 * tokens, HD), bf),
            pltpu.VMEM(proj.shape, bf),
            pltpu.VMEM((4 * tokens, width), bf),
            pltpu.VMEM((tokens, width), bf),
            pltpu.VMEM((tokens, width), bf),
            pltpu.VMEM((tokens, width), bf),
            pltpu.VMEM((tokens, width), bf),
            dma(4),
            dma(4),
            dma(8),
            dma(8),
            dma(3),
            dma(3),
            pltpu.VMEM((blocks * tokens, width + coeffs.shape[1]), bf),
            pltpu.VMEM((blocks * tokens, width), bf),
            pltpu.VMEM((2 * n_sub * tokens, width), bf),
            pltpu.VMEM((n_sub * tokens, width), bf),
            pltpu.VMEM((n_sub * tokens, width), bf),
            pltpu.VMEM((n_sub * tokens, width), bf),
            pltpu.VMEM((tokens // 2, width), bf),
            pltpu.VMEM(w_gate.shape, bf),
            pltpu.VMEM(w_up.shape, bf),
            pltpu.VMEM(w_down.shape, bf),
            dma(7),
            dma(2 * blocks),
            dma(2 * n_sub),
            dma(2 * n_sub),
            dma(2 * n_sub),
            dma(2 * n_sub),
            dma(2 * n_sub),
            dma(2 * n_sub),
            dma(2 * n_sub),
            dma(2 * n_sub),
            dma(2 * n_sub),
            dma(2 * n_sub),
            dma(2 * n_sub),
            dma(2 * n_sub),
            dma(2 * n_sub),
            dma(2),
            dma(1),
        ],
        compiler_params=pltpu.CompilerParams(
            collective_id=0, has_side_effects=True, vmem_limit_bytes=60 * 2**20
        ),
        name="layer",
    )(queries, keys, values, residual, proj, gain, coeffs, w_gate, w_up, w_down)


def per_device_dense(
    query_rows,
    key_rows,
    value_rows,
    residual_in,
    out_proj,
    norm_gain,
    expert_ids,
    gate_weights,
    expert_gate,
    expert_up,
    expert_down,
):
    n_seq = lax.axis_size("seq")
    n_sub = lax.axis_size("sub")
    experts = n_seq * n_sub
    chosen = expert_ids[0][:, :, None] == jnp.arange(experts, dtype=jnp.int32)[None, None, :]
    coeffs_local = jnp.sum(
        jnp.where(chosen, gate_weights[0].astype(jnp.float32)[:, :, None], 0.0), axis=1
    ).astype(jnp.bfloat16)

    lanes = 128 * ((experts + 127) // 128)
    coeffs = jnp.pad(coeffs_local, ((0, 0), (0, lanes - experts)))
    return layer(
        query_rows[0],
        key_rows[0],
        value_rows[0],
        residual_in[0],
        out_proj,
        norm_gain[None],
        coeffs,
        expert_gate[0],
        expert_up[0],
        expert_down[0],
        n_sub,
    )[None]


def per_device(*args):
    tokens = args[0].shape[1]
    topk = args[6].shape[2]
    n_seq = lax.axis_size("seq")
    experts = n_seq * lax.axis_size("sub")
    cap = max(2, (5 * tokens * topk + 4 * experts - 1) // (4 * experts))
    if 2 * cap >= tokens and n_seq == 4 and lax.axis_size("sub") in (4, 6, 8):
        return per_device_dense(*args)
    return per_device_routed(*args)


def solution(mesh):
    placed = (
        P(("grp", "sub"), "seq", None),
        P(("grp", "sub"), "seq", None),
        P(("grp", "sub"), "seq", None),
        P(("grp", "sub"), "seq", None),
        P("seq", None),
        P(),
        P(("grp", "sub"), "seq", None),
        P(("grp", "sub"), "seq", None),
        P(("seq", "sub"), None, None),
        P(("seq", "sub"), None, None),
        P(("seq", "sub"), None, None),
    )
    return jax.shard_map(
        per_device,
        mesh=mesh,
        in_specs=placed,
        out_specs=P(("grp", "sub"), "seq", None),
        check_vma=False,
    )
```

profile of v0, /device:TPU:0, one launch (start us, length us, event | category | flops | bytes accessed | tf_op | source)
XLA Modules:
  0.0 146.9 jit_solution(9664825373951919175)
XLA Ops:
  0.0 0.7 bitcast_convert_fusion
  0.7 0.7 select_reduce_fusion
  1.4 1.3 broadcast_in_dim.20.gain_ref
  2.7 0.1 copy.15
  2.8 0.6 pad.4.coeff_ref
  3.4 141.6 %layer.1 = bf16[128,2048]{1,0:T(8,128)(2,1)} custom-call(bf16[128,2048]{1,0:T(8,128)(2,1)} %bitcast.16, bf16[128,256]{1,0:T(8,128)(2,1)} %bitcast.18, bf16[128,256]{1,0:T(8,128)(2,1)} %bitcast.19, bf16[128,2048]{1,0:T(8,128)(2,1)} %bitcast.17, bf16[512,2048]{1,0:T(8,128)(2,1)} %proj_hbm.1, bf16[1,2048]{1,0:T(2,128)(2,1)} %broadcast_in_dim.20.gain_ref, ...), custom_call_target="tpu_custom_call" | custom-call | tf_op jit(solution)/shard_map/layer/pallas_call | solution.py:737
  145.1 1.9 %copy.17 = bf16[1,128,2048]{2,1,0:T(8,128)(2,1)} copy(bf16[1,128,2048]{2,1,0:T(8,128)(2,1)} %bitcast.15) | data formatting | bytes 1048576
where the time goes:
time: 147 us
  Pallas kernels  142 us (97%)
  local copies, waits for them, and re-layouts  3.92 us (3%)
    pallas_call x1, Pallas kernels, layer(): pl.pallas_call(functools.partial(layer_kernel, n_sub), in_specs=[hbm, hbm...  142 us

commit v1 on v0

--- a/solution.py
+++ b/solution.py
@@ -175,10 +175,6 @@
     return (wide + mixture).astype(jnp.bfloat16)[None]
 
 
-def nearest_order(n):
-    return [sorted(range(n), key=lambda p: (abs(p - z), p)) for z in range(n)]
-
-
 def lookup(table, i, j):
     total = 0
     for a, row in enumerate(table):
@@ -189,15 +185,64 @@
     return total
 
 
+def gather_tables(n):
+    arrivals, chunks = [], []
+    for z in range(n):
+        mate = z + 1 - 2 * (z % 2)
+        here = [(z, 0), (z, 1)]
+        for step in range(2 * n):
+            j, h = step // 2, step % 2
+            for p in (z - 1 - j, z + 1 + j):
+                if 0 <= p < n and not (p == mate and h == 1):
+                    here.append((p, h))
+        arrivals.append([2 * p + h for p, h in here])
+        ready = {}
+        for p in range(n):
+            if p != z:
+                ready[(p, 0)] = 2 * (abs(p - z) - 1) + 1
+            last = max(i for i, (q, _) in enumerate(here) if q == p)
+            ready[(p, 1)] = max(last, (2 * n - 2 if mate_step(n, z) > 3 else 3) if p == mate else 0)
+        order, left = [], sorted(ready, key=lambda item: (ready[item], item[0] == mate, item))
+        for step in range(1, 2 * n):
+            item = left.pop(0)
+            assert ready[item] <= step
+            order.append(2 * item[0] + item[1])
+        chunks.append(order)
+    return arrivals, chunks
+
+
+def mate_step(n, z):
+    mate = z + 1 - 2 * (z % 2)
+    corner = z == 0 or z == n - 1
+    return 2 * n - 2 if corner else 3
+
+
+def return_tables(n):
+    across = [[(2, 0), (3, 0), (3, 1), (2, 1), (1, 0), (0, 0)], [(0, 0), (2, 0), (3, 0), (3, 1), (2, 1), (1, 0)]]
+    along = [
+        [(1, 1), (2, 0), (3, 0), (3, 1), (2, 1), (1, 0), (0, 0), (0, 1)],
+        [(2, 0), (3, 0), (0, 0), (3, 1), (2, 1), (0, 1), (1, 0), (1, 1)],
+    ]
+    pick = lambda rows: [[2 * p + h for p, h in row] for row in rows] + [
+        [2 * (n - 1 - p) + h for p, h in row] for row in reversed(rows)
+    ]
+    return pick(across), pick(along)
+
+
+def first_uses(rows):
+    return [[int(v // 2 not in [u // 2 for u in row[:i]]) for i, v in enumerate(row)] for row in rows]
+
+
 def layer_kernel(
     n_sub,
     q_hbm,
     k_hbm,
     v_hbm,
-    residual_ref,
+    residual_hbm,
     proj_hbm,
     gain_ref,
-    coeff_ref,
+    ids_ref,
+    gates_ref,
     wg_hbm,
     wu_hbm,
     wd_hbm,
@@ -206,6 +251,7 @@
     k_all,
     v_all,
     proj,
+    residual,
     partial,
     core_far,
     core_near,
@@ -217,6 +263,12 @@
     kv_recv,
     part_send,
     part_recv,
+    coef,
+    coef_send,
+    coef_recv,
+    coef_up,
+    coef_down,
+    coef_z,
     rows,
     outs,
     from_core,
@@ -249,15 +301,16 @@
     z = lax.axis_index("sub")
     y = seq // 2
     c = seq % 2
-    tokens = residual_ref.shape[0]
-    width = residual_ref.shape[1]
+    tokens = residual.shape[0]
     share = q_all.shape[1]
     heads = share // HD
     length = q_all.shape[0]
     group = QH // KVH
     half = tokens // 2
-    order = nearest_order(n_sub)
     me = seq * n_sub + z
+    tile = coef.shape[0] // (4 * n_sub)
+    y_order, chunk_order = gather_tables(n_sub)
+    across_order, along_order = return_tables(n_sub)
     high = {"sub": z + 1}
     low = {"sub": z - 1}
     across = {"seq": (1 - y) * 2 + c}
@@ -267,6 +320,7 @@
     beside = {"sub": mate}
     has_high = z < n_sub - 1
     has_low = z > 0
+    corner = jnp.logical_not(jnp.logical_and(has_low, has_high))
 
     def slot(yy, p, cc):
         return (yy * n_sub + p) * 2 + cc
@@ -284,6 +338,12 @@
             device_id_type=pl.DeviceIdType.MESH,
         )
 
+    def guarded(condition, action):
+        if condition is None:
+            action()
+        else:
+            pl.when(condition)(action)
+
     def query_part(s):
         return q_hbm.at[:, pl.ds(pl.multiple_of(s * share, share), share)]
 
@@ -292,6 +352,18 @@
 
     def token_rows(ref, s):
         return ref.at[pl.ds(pl.multiple_of(s * tokens, tokens), tokens), :]
+
+    barrier = pltpu.get_barrier_semaphore()
+    for peer in (across, partner, diagonal):
+        pl.semaphore_signal(barrier, 1, device_id=peer, device_id_type=pl.DeviceIdType.MESH)
+
+    @pl.when(has_high)
+    def _():
+        pl.semaphore_signal(barrier, 1, device_id=high, device_id_type=pl.DeviceIdType.MESH)
+
+    @pl.when(has_low)
+    def _():
+        pl.semaphore_signal(barrier, 1, device_id=low, device_id_type=pl.DeviceIdType.MESH)
 
     own_parts = [
         pltpu.make_async_copy(query_part(seq), token_rows(q_all, seq), load_sem.at[0]),
@@ -300,6 +372,7 @@
         pltpu.make_async_copy(proj_hbm, proj, load_sem.at[3]),
     ]
     loads = [
+        pltpu.make_async_copy(residual_hbm, residual, load_sem.at[7]),
         pltpu.make_async_copy(wg_hbm, wg, load_sem.at[4]),
         pltpu.make_async_copy(wu_hbm, wu, load_sem.at[5]),
         pltpu.make_async_copy(wd_hbm, wd, load_sem.at[6]),
@@ -307,22 +380,32 @@
     for load in own_parts + loads:
         load.start()
 
-    barrier = pltpu.get_barrier_semaphore()
-    pl.semaphore_signal(barrier, 1, device_id=across, device_id_type=pl.DeviceIdType.MESH)
-    pl.semaphore_signal(barrier, 1, device_id=partner, device_id_type=pl.DeviceIdType.MESH)
-
-    pl.semaphore_signal(barrier, 1, device_id=diagonal, device_id_type=pl.DeviceIdType.MESH)
-
-    @pl.when(has_high)
-    def _():
-        pl.semaphore_signal(barrier, 1, device_id=high, device_id_type=pl.DeviceIdType.MESH)
-
-    @pl.when(has_low)
-    def _():
-        pl.semaphore_signal(barrier, 1, device_id=low, device_id_type=pl.DeviceIdType.MESH)
+    lanes = 128 * ((4 * n_sub + 127) // 128)
+    lane = lax.broadcasted_iota(jnp.int32, (tokens, lanes), 1)
+    ids = ids_ref[...]
+    gates = gates_ref[...].astype(jnp.float32)
+    weights_here = jnp.zeros((tokens, lanes), jnp.float32)
+    for k in range(ids.shape[1]):
+        weights_here = weights_here + jnp.where(ids[:, k : k + 1] == lane, gates[:, k : k + 1], 0.0)
+    identity = (
+        lax.broadcasted_iota(jnp.int32, (tokens, tokens), 0)
+        == lax.broadcasted_iota(jnp.int32, (tokens, tokens), 1)
+    ).astype(jnp.float32).astype(jnp.bfloat16)
+    turned = lax.dot_general(
+        weights_here.astype(jnp.bfloat16),
+        identity,
+        (((0,), (0,)), ((), ())),
+        preferred_element_type=jnp.float32,
+    )
+
+    def coef_tile(p, s, count=1):
+        return pl.ds(pl.multiple_of((p * 4 + s) * tile, tile), count * tile)
+
+    coef[coef_tile(z, seq), :] = turned[:tile].astype(jnp.bfloat16)
 
     peers = 3 + jnp.where(has_high, 1, 0) + jnp.where(has_low, 1, 0)
-    pl.semaphore_wait(barrier, peers)
+    with jax.named_scope("BAR"):
+        pl.semaphore_wait(barrier, peers)
 
     others = (
         ((1 - y) * 2 + c, across),
@@ -351,19 +434,47 @@
             ),
         )
 
+    def coef_near(s, target):
+        here = coef.at[coef_tile(z, seq), :]
+        return remote(here, here, coef_send.at[s], coef_recv.at[seq], target)
+
     for s, target in others:
         for copy in scatter_copies(s, target):
             copy.start()
+    for s, target in others:
+        coef_near(s, target).start()
 
     def arrival(ref, s, sem):
         return remote(token_rows(ref, s), token_rows(ref, s), q_send.at[s], sem, partner)
 
+    def coef_hop(p, send, target):
+        here = coef.at[coef_tile(p, 0, 4), :]
+        return remote(here, here, send.at[p], coef_z.at[p], target)
+
+    def coef_take(p, way):
+        coef_hop(p, coef_up, high).wait_recv()
+
+        @pl.when(has_high if way > 0 else has_low)
+        def _():
+            (coef_hop(p, coef_up, high) if way > 0 else coef_hop(p, coef_down, low)).start()
+
+    def coef_step(d):
+        pl.when(z - d >= 0)(lambda: coef_take(z - d, 1))
+        pl.when(z + d < n_sub)(lambda: coef_take(z + d, -1))
+
     for load in own_parts:
         load.wait()
-    for s, _ in others:
-        arrival(k_all, s, kv_recv.at[s]).wait_recv()
-        arrival(v_all, s, kv_recv.at[4 + s]).wait_recv()
-        arrival(q_all, s, q_recv.at[s]).wait_recv()
+    with jax.named_scope("ARR"):
+        for s, _ in others:
+            arrival(k_all, s, kv_recv.at[s]).wait_recv()
+            arrival(v_all, s, kv_recv.at[4 + s]).wait_recv()
+            arrival(q_all, s, q_recv.at[s]).wait_recv()
+
+    for s, target in others:
+        there = coef.at[coef_tile(z, s), :]
+        remote(there, there, coef_send.at[s], coef_recv.at[s], target).wait_recv()
+    pl.when(has_high)(lambda: coef_hop(z, coef_up, high).start())
+    pl.when(has_low)(lambda: coef_hop(z, coef_down, low).start())
 
     far_copy = remote(
         token_rows(partial, (1 - y) * 2 + 1 - c), core_far, part_send.at[0], part_recv.at[0], partner
@@ -426,26 +537,30 @@
 
         return carry
 
-    lax.fori_loop(0, 4, attend_step, 0)
+    with jax.named_scope("ATT"):
+        lax.fori_loop(0, 4, attend_step, 0)
+    coef_step(1)
+    for load in loads:
+        load.wait()
     near_copy.wait_recv()
     own_rows = pl.ds(pl.multiple_of(seq * tokens, tokens), tokens)
     base = (
-        residual_ref[...].astype(jnp.float32)
+        residual[...].astype(jnp.float32)
         + partial[own_rows, :].astype(jnp.float32)
         + core_near[...].astype(jnp.float32)
     )
-    across_copy.wait_recv()
+    with jax.named_scope("ACR"):
+        across_copy.wait_recv()
     hidden = (base + across_near[...].astype(jnp.float32)).astype(jnp.bfloat16)
     wide_ref[...] = hidden
     wide = hidden.astype(jnp.float32)
     normed = (
         wide
         * lax.rsqrt(jnp.mean(wide * wide, axis=1, keepdims=True) + 1e-06)
-        * gain_ref[...].astype(jnp.float32)
+        * gain_ref[...].astype(jnp.float32)[None, :]
     ).astype(jnp.bfloat16)
     own_slot = pl.ds(pl.multiple_of(slot(y, z, c) * tokens, tokens), tokens)
-    rows[own_slot, :width] = normed
-    rows[own_slot, width:] = coeff_ref[...]
+    rows[own_slot, :] = normed
 
     def row_copy(index, h, send, target):
         here = piece(rows, index, h)
@@ -469,13 +584,7 @@
 
     def spread(p, h):
         for condition, copy in column_copies(p, h):
-            if condition is None:
-                copy.start()
-            else:
-
-                @pl.when(condition)
-                def _():
-                    copy.start()
+            guarded(condition, copy.start)
 
     def relay_copy(p, h):
         return row_copy(slot(1 - y, p, c), h, relay_send.at[p * 2 + h], partner)
@@ -487,78 +596,82 @@
         dst = from_core.at[pl.ds(pl.multiple_of(pair * tokens, tokens), tokens), :]
         return remote(src, dst, result_send.at[pair], core_recv.at[pair], partner)
 
+    mine = (
+        lax.broadcasted_iota(jnp.int32, (2 * tile, 128), 0) % tile == me
+    ).astype(jnp.float32).astype(jnp.bfloat16)
+
     def compute(yy, p):
         wait_rows(slot(yy, p, 1 - c), 0)
         wait_rows(slot(yy, p, 1 - c), 1)
-        at = pl.ds(pl.multiple_of((yy * n_sub + p) * 2 * tokens, 2 * tokens), 2 * tokens)
-        x = rows[at, :width]
-        gains = rows[at, width:].astype(jnp.float32)
-        lane = lax.broadcasted_iota(jnp.int32, gains.shape, 1)
-        coeff = jnp.sum(jnp.where(lane == me, gains, 0.0), axis=1, keepdims=True)
-        gate = jnp.dot(x, wg[...], preferred_element_type=jnp.float32)
-        up = jnp.dot(x, wu[...], preferred_element_type=jnp.float32)
-        inner = (gate / (1.0 + jnp.exp(-gate)) * up).astype(jnp.bfloat16)
-        out = jnp.dot(inner, wd[...], preferred_element_type=jnp.float32)
-        outs[at, :] = (out * coeff).astype(jnp.bfloat16)
+        with jax.named_scope("C"):
+            at = pl.ds(pl.multiple_of((yy * n_sub + p) * 2 * tokens, 2 * tokens), 2 * tokens)
+            x = rows[at, :]
+            gains = [
+                lax.dot_general(
+                    coef[coef_tile(p, 2 * yy + cc), :],
+                    mine[:tile],
+                    (((0,), (0,)), ((), ())),
+                    preferred_element_type=jnp.float32,
+                )
+                for cc in range(2)
+            ]
+            coeff = jnp.concatenate(gains, axis=0)[:, :1]
+            gate = jnp.dot(x, wg[...], preferred_element_type=jnp.float32)
+            up = jnp.dot(x, wu[...], preferred_element_type=jnp.float32)
+            inner = (gate / (1.0 + jnp.exp(-gate)) * up).astype(jnp.bfloat16)
+            out = jnp.dot(inner, wd[...], preferred_element_type=jnp.float32)
+            outs[at, :] = (out * coeff).astype(jnp.bfloat16)
         result_copy(yy, p).start()
-
-    for load in loads:
-        load.wait()
 
     def mate_rows():
         return row_copy(slot(1 - y, z, c), 1, mate_send.at[0], beside)
 
+    spread(z, 0)
+    spread(z, 1)
+    coef_step(2)
+    compute(y, z)
+
+    def take(p, h):
+        wait_rows(slot(y, p, c), h)
+        spread(p, h)
+
+    def compute_next(k):
+        chunk = lookup(chunk_order, z, k)
+        compute(jnp.where(chunk % 2 == 1, 1 - y, y), chunk // 2)
+
+    steps = 2 * n_sub - 1
+
     def gather_step(k, carry):
-        t = (k + 1) // 2
-        other = k % 2
-        last = k == 2 * n_sub
-
-        @pl.when(jnp.logical_or(k == 0, jnp.logical_and(other == 1, t < n_sub)))
-        def _():
-            p = lookup(order, z, t)
-
-            @pl.when(t > 0)
-            def _():
-                wait_rows(slot(y, p, c), 0)
-
-            spread(p, 0)
-
-            @pl.when(t > 0)
-            def _():
-                wait_rows(slot(y, p, c), 1)
-
-            spread(p, 1)
-
-        @pl.when(k == 2 * n_sub - 3)
+        h = k % 2
+        below = z - 1 - k // 2
+        above = z + 1 + k // 2
+        pl.when(below >= 0)(lambda: take(below, h))
+        pl.when(above < n_sub)(lambda: take(above, h))
+        which = lookup(y_order, z, k)
+        wait_rows(slot(1 - y, which // 2, c), which % 2)
+        relay_copy(which // 2, which % 2).start()
+
+        @pl.when(k == jnp.where(corner, 1, 3))
         def _():
             mate_rows().start()
 
-        q = lookup(order, z, t - 1)
-
-        @pl.when(other == 1)
-        def _():
-            wait_rows(slot(1 - y, q, c), 0)
-            relay_copy(q, 0).start()
-
-            @pl.when(q != mate)
-            def _():
-                wait_rows(slot(1 - y, q, c), 1)
-                relay_copy(q, 1).start()
-
-        @pl.when(last)
+        @pl.when(k == jnp.where(corner, steps - 1, 3))
         def _():
             wait_rows(slot(1 - y, mate, c), 1)
             relay_copy(mate, 1).start()
 
-        @pl.when(jnp.logical_or(other == 0, q != mate))
-        def _():
-            yy = jnp.where(jnp.logical_or(other == 1, last), 1 - y, y)
-            p = jnp.where(last, mate, jnp.where(other == 1, q, lookup(order, z, t)))
-            compute(yy, p)
+        @pl.when(k == 1)
+        def _():
+            coef_step(3)
+
+        @pl.when(jnp.logical_and(k > 0, k < steps - 1))
+        def _():
+            compute_next(k - 1)
 
         return carry
 
-    lax.fori_loop(0, 2 * n_sub + 1, gather_step, 0)
+    with jax.named_scope("GATHER"):
+        lax.fori_loop(0, steps, gather_step, 0)
 
     def wide_load(ref, index, h):
         at = pl.ds(pl.multiple_of(index * tokens + h * half, half), half)
@@ -595,51 +708,53 @@
             piece(outs, slot(1 - y, p, c), 1), from_mate, mate_send.at[1], mate_recv.at[0], beside
         )
 
-    def y_step(k, carry):
-        p = lookup(order, z, n_sub - 1 - k)
-        result_copy(1 - y, p).wait_recv()
-        index = slot(1 - y, p, c)
-        for h in range(2):
-            store_out(
-                index, h, wide_load(outs, index, h) + wide_load(from_core, (1 - y) * n_sub + p, h)
-            )
-
-            @pl.when(jnp.logical_and(p == mate, h == 1))
-            def _():
-                mate_result(mate).start()
-
-            @pl.when(jnp.logical_or(p != z, h == 0) & jnp.logical_or(p != mate, h == 0))
-            def _():
-                y_copy(p, h).start()
-
+    def chip_sum(yy, p, h):
+        index = slot(yy, p, c)
+        store_out(index, h, wide_load(outs, index, h) + wide_load(from_core, yy * n_sub + p, h))
+
+    across_first = first_uses(across_order)
+    along_first = first_uses(along_order)
+
+    def send_across(k):
+        which = lookup(across_order, z, k)
+        p, h = which // 2, which % 2
+        pl.when(lookup(across_first, z, k) == 1)(lambda: result_copy(1 - y, p).wait_recv())
+        chip_sum(1 - y, p, h)
+        y_copy(p, h).start()
+
+    send_across(0)
+
+    def tail_step(k, carry):
+        compute_next(k)
         return carry
 
-    lax.fori_loop(0, n_sub, y_step, 0)
-
-    def own_step(k, carry):
-        p = lookup(order, z, n_sub - 1 - k)
-        result_copy(y, p).wait_recv()
-        index = slot(y, p, c)
-        store = wide_load(outs, index, 0) + wide_load(from_core, y * n_sub + p, 0)
-        store_out(index, 0, store)
-        store = wide_load(outs, index, 1) + wide_load(from_core, y * n_sub + p, 1)
-        store_out(index, 1, store)
+    lax.fori_loop(steps - 2, steps, tail_step, 0)
+
+    def across_step(k, carry):
+        send_across(k)
         return carry
 
-    lax.fori_loop(0, n_sub, own_step, 0)
-    mate_result(z).wait_recv()
-    store_out(
-        slot(1 - y, z, c),
-        1,
-        wide_load(outs, slot(1 - y, z, c), 1) + from_mate[...].astype(jnp.float32),
-    )
-    y_copy(z, 1).start()
-
-    def z_step(k, carry):
-        p = lookup(order, z, n_sub - 1 - k // 2)
-        h = k % 2
+    with jax.named_scope("ACROSS"):
+        lax.fori_loop(1, steps - 1, across_step, 0)
+        chip_sum(1 - y, mate, 1)
+        mate_result(mate).start()
+
+    def along_step(k, carry):
+        which = lookup(along_order, z, k)
+        p, h = which // 2, which % 2
         index = slot(y, p, c)
         direct = jnp.logical_or(p != mate, h == 0)
+
+        @pl.when(k == jnp.where(corner, 2, 4))
+        def _():
+            mate_result(z).wait_recv()
+            here = slot(1 - y, z, c)
+            chip_sum(1 - y, z, 1)
+            store_out(here, 1, wide_load(outs, here, 1) + from_mate[...].astype(jnp.float32))
+            y_copy(z, 1).start()
+
+        pl.when(lookup(along_first, z, k) == 1)(lambda: result_copy(y, p).wait_recv())
+        chip_sum(y, p, h)
 
         @pl.when(direct)
         def _():
@@ -667,6 +782,7 @@
         @pl.when(p == z)
         def _():
             at = pl.ds(pl.multiple_of(h * half, half), half)
+
             @pl.when(has_low)
             def _():
                 up_copy(p, h).wait_recv()
@@ -683,35 +799,25 @@
 
         return carry
 
-    lax.fori_loop(0, 2 * n_sub, z_step, 0)
+    with jax.named_scope("ALONG"):
+        lax.fori_loop(0, 2 * n_sub, along_step, 0)
 
     def drain(k, carry):
         p = k // 2
         h = k % 2
         for condition, copy in column_copies(p, h):
-            if condition is None:
-                copy.wait_send()
-            else:
-
-                @pl.when(condition)
-                def _():
-                    copy.wait_send()
+            guarded(condition, copy.wait_send)
 
         relay_copy(p, h).wait_send()
-
-        @pl.when(jnp.logical_or(p != mate, h == 0))
-        def _():
-            y_copy(p, h).wait_send()
-
+        pl.when(jnp.logical_or(p != mate, h == 0))(lambda: y_copy(p, h).wait_send())
         result_copy(h, p).wait_send()
-
-        @pl.when(p > z)
-        def _():
-            up_copy(p, h).wait_send()
-
-        @pl.when(p < z)
-        def _():
-            down_copy(p, h).wait_send()
+        pl.when(p > z)(lambda: up_copy(p, h).wait_send())
+        pl.when(p < z)(lambda: down_copy(p, h).wait_send())
+
+        @pl.when(h == 0)
+        def _():
+            pl.when(jnp.logical_and(p <= z, has_high))(lambda: coef_hop(p, coef_up, high).wait_send())
+            pl.when(jnp.logical_and(p >= z, has_low))(lambda: coef_hop(p, coef_down, low).wait_send())
 
         return carry
 
@@ -719,6 +825,7 @@
     for s, target in others:
         for copy in scatter_copies(s, target):
             copy.wait_send()
+        coef_near(s, target).wait_send()
     mate_rows().wait_send()
     mate_result(mate).wait_send()
     far_copy.wait_send()
@@ -726,17 +833,18 @@
     near_copy.wait_send()
 
 
-def layer(queries, keys, values, residual, proj, gain, coeffs, w_gate, w_up, w_down, n_sub):
+def layer(queries, keys, values, residual, proj, gain, ids, gates, w_gate, w_up, w_down, n_sub):
     tokens, width = residual.shape
     share = proj.shape[0]
     blocks = 4 * n_sub
+    tile = 16 * ((blocks + 15) // 16)
     dma = lambda count: pltpu.SemaphoreType.DMA((count,))
     hbm = pl.BlockSpec(memory_space=pl.ANY)
     vmem = pl.BlockSpec(memory_space=pltpu.VMEM)
     bf = jnp.bfloat16
     return pl.pallas_call(
         functools.partial(layer_kernel, n_sub),
-        in_specs=[hbm, hbm, hbm, vmem, hbm, vmem, vmem, hbm, hbm, hbm],
+        in_specs=[hbm, hbm, hbm, hbm, hbm, vmem, vmem, vmem, hbm, hbm, hbm],
         out_specs=vmem,
         out_shape=jax.ShapeDtypeStruct((tokens, width), bf),
         scratch_shapes=[
@@ -744,6 +852,7 @@
             pltpu.VMEM((4 * tokens, HD), bf),
             pltpu.VMEM((4 * tokens, HD), bf),
             pltpu.VMEM(proj.shape, bf),
+            pltpu.VMEM((tokens, width), bf),
             pltpu.VMEM((4 * tokens, width), bf),
             pltpu.VMEM((tokens, width), bf),
             pltpu.VMEM((tokens, width), bf),
@@ -755,7 +864,13 @@
             dma(8),
             dma(3),
             dma(3),
-            pltpu.VMEM((blocks * tokens, width + coeffs.shape[1]), bf),
+            pltpu.VMEM((blocks * tile, tokens), bf),
+            dma(4),
+            dma(4),
+            dma(n_sub),
+            dma(n_sub),
+            dma(n_sub),
+            pltpu.VMEM((blocks * tokens, width), bf),
             pltpu.VMEM((blocks * tokens, width), bf),
             pltpu.VMEM((2 * n_sub * tokens, width), bf),
             pltpu.VMEM((n_sub * tokens, width), bf),
@@ -765,7 +880,7 @@
             pltpu.VMEM(w_gate.shape, bf),
             pltpu.VMEM(w_up.shape, bf),
             pltpu.VMEM(w_down.shape, bf),
-            dma(7),
+            dma(8),
             dma(2 * blocks),
             dma(2 * n_sub),
             dma(2 * n_sub),
@@ -787,7 +902,7 @@
             collective_id=0, has_side_effects=True, vmem_limit_bytes=60 * 2**20
         ),
         name="layer",
-    )(queries, keys, values, residual, proj, gain, coeffs, w_gate, w_up, w_down)
+    )(queries, keys, values, residual, proj, gain, ids, gates, w_gate, w_up, w_down)
 
 
 def per_device_dense(
@@ -803,28 +918,19 @@
     expert_up,
     expert_down,
 ):
-    n_seq = lax.axis_size("seq")
-    n_sub = lax.axis_size("sub")
-    experts = n_seq * n_sub
-    chosen = expert_ids[0][:, :, None] == jnp.arange(experts, dtype=jnp.int32)[None, None, :]
-    coeffs_local = jnp.sum(
-        jnp.where(chosen, gate_weights[0].astype(jnp.float32)[:, :, None], 0.0), axis=1
-    ).astype(jnp.bfloat16)
-
-    lanes = 128 * ((experts + 127) // 128)
-    coeffs = jnp.pad(coeffs_local, ((0, 0), (0, lanes - experts)))
     return layer(
         query_rows[0],
         key_rows[0],
         value_rows[0],
         residual_in[0],
         out_proj,
-        norm_gain[None],
-        coeffs,
+        norm_gain,
+        expert_ids[0],
+        gate_weights[0],
         expert_gate[0],
         expert_up[0],
         expert_down[0],
-        n_sub,
+        lax.axis_size("sub"),
     )[None]
 
 
@@ -834,7 +940,7 @@
     n_seq = lax.axis_size("seq")
     experts = n_seq * lax.axis_size("sub")
     cap = max(2, (5 * tokens * topk + 4 * experts - 1) // (4 * experts))
-    if 2 * cap >= tokens and n_seq == 4 and lax.axis_size("sub") in (4, 6, 8):
+    if 2 * cap >= tokens and n_seq == 4 and lax.axis_size("sub") == 4 and tokens == 128:
         return per_device_dense(*args)
     return per_device_routed(*args)
 

time: 147 us -> 135 us (0.918)
  Pallas kernels: 142 us -> 130 us
    pallas_call x1, Pallas kernels: 142 us -> 130 us  [layer(): pl.pallas_call(functools.partial(layer_kernel, n_sub), in_specs=[hbm, hbm...]
    unnamed x1 -> x3, local copies, waits for them, and re-layouts: 1.88 us -> 4.68 us
where the time goes in v1:
time: 135 us
  Pallas kernels  130 us (96%)
  local copies, waits for them, and re-layouts  4.68 us (3%)
    pallas_call x1, Pallas kernels, layer(): pl.pallas_call(functools.partial(layer_kernel, n_sub), in_specs=[hbm, hbm...  130 us
    unnamed x3, local copies, waits for them, and re-layouts  4.68 us

profile of v1, /device:TPU:0, one launch (start us, length us, event | category | flops | bytes accessed | tf_op | source)
XLA Modules:
  0.0 135.0 jit_solution(15524343942759912441)
XLA Ops:
  0.0 1.4 %copy.13 = bf16[1,128,8]{2,1,0:T(8,128)(2,1)} copy(bf16[1,128,8]{1,2,0:T(8,128)(2,1)} %param.18) | data formatting | bytes 4096 | tf_op args[7]
  1.4 1.4 %copy.12 = s32[1,128,8]{2,1,0:T(8,128)} copy(s32[1,128,8]{1,2,0:T(8,128)} %param.17) | data formatting | bytes 8192 | tf_op args[6]
  2.8 130.3 %layer.1 = bf16[128,2048]{1,0:T(8,128)(2,1)} custom-call(bf16[128,2048]{1,0:T(8,128)(2,1)} %bitcast.14, bf16[128,256]{1,0:T(8,128)(2,1)} %bitcast.18, bf16[128,256]{1,0:T(8,128)(2,1)} %bitcast.19, bf16[128,2048]{1,0:T(8,128)(2,1)} %bitcast.15, bf16[512,2048]{1,0:T(8,128)(2,1)} %proj_hbm.1, bf16[2048]{0:T(1024)(128)(2,1)} %gain_ref.1, s32[128,8]{1,0:T(8,128)} %bitcast.16, ...), custom_call_target="tpu_custom_call" | custom-call | tf_op jit(solution)/shard_map/layer/pallas_call | solution.py:845
  133.1 1.9 %copy.15 = bf16[1,128,2048]{2,1,0:T(8,128)(2,1)} copy(bf16[1,128,2048]{2,1,0:T(8,128)(2,1)} %bitcast.13) | data formatting | bytes 1048576

commit v2 on v1

--- a/solution.py
+++ b/solution.py
@@ -175,62 +175,70 @@
     return (wide + mixture).astype(jnp.bfloat16)[None]
 
 
-def lookup(table, i, j):
-    total = 0
-    for a, row in enumerate(table):
-        for b, value in enumerate(row):
-            if value:
-                hit = jnp.logical_and(i == a, j == b)
-                total = total + jnp.where(hit, value, 0)
-    return total
-
-
-def gather_tables(n):
-    arrivals, chunks = [], []
-    for z in range(n):
-        mate = z + 1 - 2 * (z % 2)
-        here = [(z, 0), (z, 1)]
-        for step in range(2 * n):
-            j, h = step // 2, step % 2
-            for p in (z - 1 - j, z + 1 + j):
-                if 0 <= p < n and not (p == mate and h == 1):
-                    here.append((p, h))
-        arrivals.append([2 * p + h for p, h in here])
-        ready = {}
-        for p in range(n):
-            if p != z:
-                ready[(p, 0)] = 2 * (abs(p - z) - 1) + 1
-            last = max(i for i, (q, _) in enumerate(here) if q == p)
-            ready[(p, 1)] = max(last, (2 * n - 2 if mate_step(n, z) > 3 else 3) if p == mate else 0)
-        order, left = [], sorted(ready, key=lambda item: (ready[item], item[0] == mate, item))
-        for step in range(1, 2 * n):
-            item = left.pop(0)
-            assert ready[item] <= step
-            order.append(2 * item[0] + item[1])
-        chunks.append(order)
-    return arrivals, chunks
-
-
-def mate_step(n, z):
-    mate = z + 1 - 2 * (z % 2)
-    corner = z == 0 or z == n - 1
-    return 2 * n - 2 if corner else 3
-
-
-def return_tables(n):
-    across = [[(2, 0), (3, 0), (3, 1), (2, 1), (1, 0), (0, 0)], [(0, 0), (2, 0), (3, 0), (3, 1), (2, 1), (1, 0)]]
-    along = [
-        [(1, 1), (2, 0), (3, 0), (3, 1), (2, 1), (1, 0), (0, 0), (0, 1)],
-        [(2, 0), (3, 0), (0, 0), (3, 1), (2, 1), (0, 1), (1, 0), (1, 1)],
-    ]
-    pick = lambda rows: [[2 * p + h for p, h in row] for row in rows] + [
-        [2 * (n - 1 - p) + h for p, h in row] for row in reversed(rows)
-    ]
-    return pick(across), pick(along)
-
-
-def first_uses(rows):
-    return [[int(v // 2 not in [u // 2 for u in row[:i]]) for i, v in enumerate(row)] for row in rows]
+PLAN = [
+    [
+        ("C", 0, 0), ("T", 1, 0), ("Y", 0, 0), ("T", 1, 1), ("Y", 0, 1), ("R", 0, 0),
+        ("C", 1, 0), ("C", 0, 1), ("T", 2, 0), ("Y", 1, 0), ("A", 1, 0), ("A", 1, 2),
+        ("T", 2, 1), ("C", 2, 0), ("Y", 2, 0), ("T", 3, 0), ("A", 2, 0), ("Y", 2, 1),
+        ("A", 2, 1), ("C", 2, 1), ("T", 3, 1), ("A", 2, 2), ("C", 3, 0), ("Y", 3, 0),
+        ("M", 2, 0), ("Y", 1, 1), ("S", 2, 3), ("C", 1, 1), ("Y", 3, 1), ("M", 2, 1),
+        ("S", 0, 0), ("C", 3, 1), ("M", 2, 2), ("S", 1, 1), ("A", 2, 3), ("S", 3, 0),
+        ("M", 1, 0), ("S", 3, 1), ("A", 3, 0), ("S", 3, 2), ("A", 3, 1), ("S", 3, 3),
+        ("A", 3, 2), ("S", 1, 3), ("A", 3, 3), ("S", 0, 1), ("M", 1, 2), ("S", 0, 2),
+        ("A", 0, 0), ("A", 1, 1), ("S", 0, 3), ("A", 0, 1), ("A", 1, 3), ("A", 0, 2),
+        ("A", 0, 3),
+    ],
+    [
+        ("C", 1, 0), ("T", 0, 0), ("T", 2, 0), ("Y", 1, 0), ("T", 0, 1), ("T", 2, 1),
+        ("Y", 1, 1), ("C", 0, 0), ("C", 1, 1), ("T", 3, 0), ("Y", 0, 0), ("Y", 0, 1),
+        ("C", 2, 0), ("C", 0, 1), ("T", 3, 1), ("Y", 2, 0), ("R", 0, 0), ("C", 3, 0),
+        ("Y", 2, 1), ("C", 2, 1), ("M", 2, 3), ("Y", 3, 0), ("A", 2, 1), ("M", 0, 2),
+        ("S", 0, 0), ("A", 2, 2), ("Y", 3, 1), ("S", 0, 1), ("C", 3, 1), ("S", 2, 0),
+        ("M", 3, 3), ("S", 3, 0), ("M", 2, 1), ("S", 3, 1), ("A", 2, 0), ("S", 3, 2),
+        ("M", 2, 2), ("S", 0, 3), ("A", 2, 3), ("S", 1, 0), ("A", 3, 0), ("S", 1, 1),
+        ("A", 1, 0), ("A", 3, 1), ("S", 1, 3), ("A", 0, 0), ("A", 3, 2), ("A", 0, 1),
+        ("A", 3, 3), ("A", 0, 2), ("S", 1, 2), ("A", 0, 3), ("A", 1, 1), ("A", 1, 2),
+        ("A", 1, 3),
+    ],
+]
+CODES = "TYRCSMA"
+
+
+def encode_plan():
+    n = len(PLAN)
+    moved = [{(p, q) for what, p, q in steps if what == "M"} for steps in PLAN]
+    table = []
+    for here, steps in enumerate(PLAN):
+        met, row = set(), []
+        for what, p, q in steps:
+            first = one = two = 0
+            if what in "SMA":
+                key = (what == "A", p)
+                first = int(key not in met)
+                met.add(key)
+            if what == "A":
+                one = int((p, q) not in moved[here])
+            elif what in "SM":
+                one = int(here == 1 and p >= 1 and (p, q) in moved[0])
+                if here == 1:
+                    two = int(p <= 1 and (3 - p, q) in moved[1])
+                else:
+                    two = int(p == 0 and (p, q) in moved[1])
+            code = CODES.index(what)
+            row.append((((((code * 4 + p) * 4 + q) * 2 + first) * 2) + one) * 2 + two)
+        table.append(row)
+    assert n == 2 and len(table[0]) == len(table[1])
+    return table
+
+
+def fetch(table, first_row, k):
+    word = 0
+    for w in range(0, len(table[0]), 3):
+        pair = [sum(v * 1024**i for i, v in enumerate(row[w : w + 3])) for row in table]
+        word = jnp.where(k // 3 == w // 3, jnp.where(first_row, pair[0], pair[1]), word)
+    third = k % 3
+    word = jnp.where(third == 0, word, jnp.where(third == 1, word // 1024, word // 1024**2))
+    return word % 1024
 
 
 def layer_kernel(
@@ -273,9 +281,8 @@
     outs,
     from_core,
     from_y,
-    from_low,
-    from_high,
-    from_mate,
+    from_line,
+    from_moved,
     wg,
     wu,
     wd,
@@ -290,12 +297,11 @@
     result_send,
     y_recv,
     result_y_send,
-    low_recv,
-    high_recv,
-    result_up_send,
-    result_down_send,
+    line_recv,
+    line_send,
+    moved_recv,
+    moved_send,
     mate_send,
-    mate_recv,
 ):
     seq = lax.axis_index("seq")
     z = lax.axis_index("sub")
@@ -309,8 +315,8 @@
     half = tokens // 2
     me = seq * n_sub + z
     tile = coef.shape[0] // (4 * n_sub)
-    y_order, chunk_order = gather_tables(n_sub)
-    across_order, along_order = return_tables(n_sub)
+    quarter = tokens // 4
+    plan = encode_plan()
     high = {"sub": z + 1}
     low = {"sub": z - 1}
     across = {"seq": (1 - y) * 2 + c}
@@ -321,6 +327,7 @@
     has_high = z < n_sub - 1
     has_low = z > 0
     corner = jnp.logical_not(jnp.logical_and(has_low, has_high))
+    mirrored = jnp.where(z >= n_sub // 2, 1, 0)
 
     def slot(yy, p, cc):
         return (yy * n_sub + p) * 2 + cc
@@ -439,10 +446,10 @@
         return remote(here, here, coef_send.at[s], coef_recv.at[seq], target)
 
     for s, target in others:
+        coef_near(s, target).start()
+    for s, target in others:
         for copy in scatter_copies(s, target):
             copy.start()
-    for s, target in others:
-        coef_near(s, target).start()
 
     def arrival(ref, s, sem):
         return remote(token_rows(ref, s), token_rows(ref, s), q_send.at[s], sem, partner)
@@ -542,6 +549,7 @@
     coef_step(1)
     for load in loads:
         load.wait()
+    coef_step(2)
     near_copy.wait_recv()
     own_rows = pl.ds(pl.multiple_of(seq * tokens, tokens), tokens)
     base = (
@@ -628,179 +636,123 @@
 
     spread(z, 0)
     spread(z, 1)
-    coef_step(2)
-    compute(y, z)
-
-    def take(p, h):
-        wait_rows(slot(y, p, c), h)
-        spread(p, h)
-
-    def compute_next(k):
-        chunk = lookup(chunk_order, z, k)
-        compute(jnp.where(chunk % 2 == 1, 1 - y, y), chunk // 2)
-
-    steps = 2 * n_sub - 1
-
-    def gather_step(k, carry):
-        h = k % 2
-        below = z - 1 - k // 2
-        above = z + 1 + k // 2
-        pl.when(below >= 0)(lambda: take(below, h))
-        pl.when(above < n_sub)(lambda: take(above, h))
-        which = lookup(y_order, z, k)
-        wait_rows(slot(1 - y, which // 2, c), which % 2)
-        relay_copy(which // 2, which % 2).start()
-
-        @pl.when(k == jnp.where(corner, 1, 3))
-        def _():
-            mate_rows().start()
-
-        @pl.when(k == jnp.where(corner, steps - 1, 3))
-        def _():
-            wait_rows(slot(1 - y, mate, c), 1)
-            relay_copy(mate, 1).start()
-
-        @pl.when(k == 1)
-        def _():
-            coef_step(3)
-
-        @pl.when(jnp.logical_and(k > 0, k < steps - 1))
-        def _():
-            compute_next(k - 1)
-
-        return carry
-
-    with jax.named_scope("GATHER"):
-        lax.fori_loop(0, steps, gather_step, 0)
-
-    def wide_load(ref, index, h):
-        at = pl.ds(pl.multiple_of(index * tokens + h * half, half), half)
-        return ref[at, :].astype(jnp.float32)
-
-    def y_copy(p, h):
-        at = p * 2 + h
+    coef_step(3)
+
+    def part(index, q):
+        return pl.ds(pl.multiple_of(index * tokens + q * quarter, quarter), quarter)
+
+    def y_copy(p, q):
+        at = p * 4 + q
         return remote(
-            piece(outs, slot(1 - y, p, c), h),
-            piece(from_y, p, h),
+            outs.at[part(slot(1 - y, p, c), q), :],
+            from_y.at[part(p, q), :],
             result_y_send.at[at],
             y_recv.at[at],
             across,
         )
 
-    def z_copy(p, h, buffer, send, recv, target):
-        at = p * 2 + h
+    def passed(yy, p, q, way, buffer, send, recv):
+        at = p * 4 + q
         return remote(
-            piece(outs, slot(y, p, c), h), piece(buffer, p, h), send.at[at], recv.at[at], target
+            outs.at[part(slot(yy, p, c), q), :],
+            buffer.at[part(way * n_sub + p, q), :],
+            send.at[at],
+            recv.at[way * 4 * n_sub + at],
+            {"sub": z + 1 - 2 * way},
         )
 
-    def up_copy(p, h):
-        return z_copy(p, h, from_low, result_up_send, low_recv, high)
-
-    def down_copy(p, h):
-        return z_copy(p, h, from_high, result_down_send, high_recv, low)
-
-    def store_out(index, h, value):
-        at = pl.ds(pl.multiple_of(index * tokens + h * half, half), half)
-        outs[at, :] = value.astype(jnp.bfloat16)
-
-    def mate_result(p):
-        return remote(
-            piece(outs, slot(1 - y, p, c), 1), from_mate, mate_send.at[1], mate_recv.at[0], beside
-        )
-
-    def chip_sum(yy, p, h):
-        index = slot(yy, p, c)
-        store_out(index, h, wide_load(outs, index, h) + wide_load(from_core, yy * n_sub + p, h))
-
-    across_first = first_uses(across_order)
-    along_first = first_uses(along_order)
-
-    def send_across(k):
-        which = lookup(across_order, z, k)
-        p, h = which // 2, which % 2
-        pl.when(lookup(across_first, z, k) == 1)(lambda: result_copy(1 - y, p).wait_recv())
-        chip_sum(1 - y, p, h)
-        y_copy(p, h).start()
-
-    send_across(0)
-
-    def tail_step(k, carry):
-        compute_next(k)
+    def line_copy(p, q, way):
+        return passed(y, p, q, way, from_line, line_send, line_recv)
+
+    def moved_copy(p, q, way):
+        return passed(1 - y, p, q, way, from_moved, moved_send, moved_recv)
+
+    def add_to(index, q, ref, at, q_at):
+        here = part(index, q)
+        total = outs[here, :].astype(jnp.float32) + ref[part(at, q_at), :].astype(jnp.float32)
+        outs[here, :] = total.astype(jnp.bfloat16)
+
+    def toward(p):
+        return jnp.where(p > z, 0, 1)
+
+    def act(k, carry):
+        entry = fetch(plan, corner, k)
+        what = entry // 128
+        place = entry // 32 % 4
+        q = entry // 8 % 4
+        first = entry // 4 % 2
+        one = entry // 2 % 2
+        two = entry % 2
+        p = jnp.where(mirrored == 1, n_sub - 1 - place, place)
+
+        @pl.when(what == CODES.index("T"))
+        def _():
+            wait_rows(slot(y, p, c), q)
+            spread(p, q)
+
+        @pl.when(what == CODES.index("Y"))
+        def _():
+            wait_rows(slot(1 - y, p, c), q)
+            relay_copy(p, q).start()
+
+        @pl.when(what == CODES.index("R"))
+        def _():
+            mate_rows().start()
+
+        @pl.when(what == CODES.index("C"))
+        def _():
+            compute(jnp.where(q == 1, 1 - y, y), p)
+
+        @pl.when(jnp.logical_or(what == CODES.index("S"), what == CODES.index("M")))
+        def _():
+            index = slot(1 - y, p, c)
+            pl.when(first == 1)(lambda: result_copy(1 - y, p).wait_recv())
+            add_to(index, q, from_core, (1 - y) * n_sub + p, q)
+
+            @pl.when(one == 1)
+            def _():
+                moved_copy(p, q, mirrored).wait_recv()
+                add_to(index, q, from_moved, mirrored * n_sub + p, q)
+
+            @pl.when(two == 1)
+            def _():
+                moved_copy(p, q, 1 - mirrored).wait_recv()
+                add_to(index, q, from_moved, (1 - mirrored) * n_sub + p, q)
+
+            pl.when(what == CODES.index("S"))(lambda: y_copy(p, q).start())
+            pl.when(what == CODES.index("M"))(lambda: moved_copy(p, q, toward(p)).start())
+
+        @pl.when(what == CODES.index("A"))
+        def _():
+            index = slot(y, p, c)
+            pl.when(first == 1)(lambda: result_copy(y, p).wait_recv())
+            add_to(index, q, from_core, y * n_sub + p, q)
+
+            @pl.when(one == 1)
+            def _():
+                y_copy(p, q).wait_recv()
+                add_to(index, q, from_y, p, q)
+
+            for way, comes in ((0, p >= z), (1, p <= z)):
+
+                @pl.when(jnp.logical_and(comes, has_low if way == 0 else has_high))
+                def _():
+                    line_copy(p, q, way).wait_recv()
+                    add_to(index, q, from_line, way * n_sub + p, q)
+
+            pl.when(p != z)(lambda: line_copy(p, q, toward(p)).start())
+
+            @pl.when(p == z)
+            def _():
+                at = part(0, q)
+                o_ref[at, :] = (
+                    wide_ref[at, :].astype(jnp.float32) + outs[part(index, q), :].astype(jnp.float32)
+                ).astype(jnp.bfloat16)
+
         return carry
 
-    lax.fori_loop(steps - 2, steps, tail_step, 0)
-
-    def across_step(k, carry):
-        send_across(k)
-        return carry
-
-    with jax.named_scope("ACROSS"):
-        lax.fori_loop(1, steps - 1, across_step, 0)
-        chip_sum(1 - y, mate, 1)
-        mate_result(mate).start()
-
-    def along_step(k, carry):
-        which = lookup(along_order, z, k)
-        p, h = which // 2, which % 2
-        index = slot(y, p, c)
-        direct = jnp.logical_or(p != mate, h == 0)
-
-        @pl.when(k == jnp.where(corner, 2, 4))
-        def _():
-            mate_result(z).wait_recv()
-            here = slot(1 - y, z, c)
-            chip_sum(1 - y, z, 1)
-            store_out(here, 1, wide_load(outs, here, 1) + from_mate[...].astype(jnp.float32))
-            y_copy(z, 1).start()
-
-        pl.when(lookup(along_first, z, k) == 1)(lambda: result_copy(y, p).wait_recv())
-        chip_sum(y, p, h)
-
-        @pl.when(direct)
-        def _():
-            y_copy(p, h).wait_recv()
-            store_out(index, h, wide_load(outs, index, h) + wide_load(from_y, p, h))
-
-        @pl.when(p > z)
-        def _():
-            @pl.when(has_low)
-            def _():
-                up_copy(p, h).wait_recv()
-                store_out(index, h, wide_load(outs, index, h) + wide_load(from_low, p, h))
-
-            up_copy(p, h).start()
-
-        @pl.when(p < z)
-        def _():
-            @pl.when(has_high)
-            def _():
-                down_copy(p, h).wait_recv()
-                store_out(index, h, wide_load(outs, index, h) + wide_load(from_high, p, h))
-
-            down_copy(p, h).start()
-
-        @pl.when(p == z)
-        def _():
-            at = pl.ds(pl.multiple_of(h * half, half), half)
-
-            @pl.when(has_low)
-            def _():
-                up_copy(p, h).wait_recv()
-                store_out(index, h, wide_load(outs, index, h) + wide_load(from_low, p, h))
-
-            @pl.when(has_high)
-            def _():
-                down_copy(p, h).wait_recv()
-                store_out(index, h, wide_load(outs, index, h) + wide_load(from_high, p, h))
-
-            o_ref[at, :] = (wide_ref[at, :].astype(jnp.float32) + wide_load(outs, index, h)).astype(
-                jnp.bfloat16
-            )
-
-        return carry
-
-    with jax.named_scope("ALONG"):
-        lax.fori_loop(0, 2 * n_sub, along_step, 0)
+    with jax.named_scope("PLAN"):
+        lax.fori_loop(0, len(plan[0]), act, 0)
 
     def drain(k, carry):
         p = k // 2
@@ -809,10 +761,7 @@
             guarded(condition, copy.wait_send)
 
         relay_copy(p, h).wait_send()
-        pl.when(jnp.logical_or(p != mate, h == 0))(lambda: y_copy(p, h).wait_send())
         result_copy(h, p).wait_send()
-        pl.when(p > z)(lambda: up_copy(p, h).wait_send())
-        pl.when(p < z)(lambda: down_copy(p, h).wait_send())
 
         @pl.when(h == 0)
         def _():
@@ -822,12 +771,24 @@
         return carry
 
     lax.fori_loop(0, 2 * n_sub, drain, 0)
+    for here, steps in enumerate(PLAN):
+
+        @pl.when(corner == (here == 0))
+        def _():
+            for what, place, q in steps:
+                p = jnp.where(mirrored == 1, n_sub - 1 - place, place)
+                if what == "S":
+                    y_copy(p, q).wait_send()
+                elif what == "M":
+                    moved_copy(p, q, toward(p)).wait_send()
+                elif what == "A" and place != here:
+                    line_copy(p, q, toward(p)).wait_send()
+
     for s, target in others:
         for copy in scatter_copies(s, target):
             copy.wait_send()
         coef_near(s, target).wait_send()
     mate_rows().wait_send()
-    mate_result(mate).wait_send()
     far_copy.wait_send()
     across_copy.wait_send()
     near_copy.wait_send()
@@ -874,9 +835,8 @@
             pltpu.VMEM((blocks * tokens, width), bf),
             pltpu.VMEM((2 * n_sub * tokens, width), bf),
             pltpu.VMEM((n_sub * tokens, width), bf),
-            pltpu.VMEM((n_sub * tokens, width), bf),
-            pltpu.VMEM((n_sub * tokens, width), bf),
-            pltpu.VMEM((tokens // 2, width), bf),
+            pltpu.VMEM((2 * n_sub * tokens, width), bf),
+            pltpu.VMEM((2 * n_sub * tokens, width), bf),
             pltpu.VMEM(w_gate.shape, bf),
             pltpu.VMEM(w_up.shape, bf),
             pltpu.VMEM(w_down.shape, bf),
@@ -889,13 +849,12 @@
             dma(2 * n_sub),
             dma(2 * n_sub),
             dma(2 * n_sub),
-            dma(2 * n_sub),
-            dma(2 * n_sub),
-            dma(2 * n_sub),
-            dma(2 * n_sub),
-            dma(2 * n_sub),
-            dma(2 * n_sub),
-            dma(2),
+            dma(4 * n_sub),
+            dma(4 * n_sub),
+            dma(8 * n_sub),
+            dma(4 * n_sub),
+            dma(8 * n_sub),
+            dma(4 * n_sub),
             dma(1),
         ],
         compiler_params=pltpu.CompilerParams(

time: 135 us -> 125 us (0.926)
  Pallas kernels: 130 us -> 120 us
    pallas_call x1, Pallas kernels: 130 us -> 120 us  [layer(): pl.pallas_call(functools.partial(layer_kernel, n_sub), in_specs=[hbm, hbm...]
where the time goes in v2:
time: 125 us; the launch traced here: 124 us
  Pallas kernels  120 us (96%)
  local copies, waits for them, and re-layouts  4.68 us (4%)
    pallas_call x1, Pallas kernels, layer(): pl.pallas_call(functools.partial(layer_kernel, n_sub), in_specs=[hbm, hbm...  120 us
    unnamed x3, local copies, waits for them, and re-layouts  4.68 us

profile of v2, /device:TPU:0, one launch (start us, length us, event | category | flops | bytes accessed | tf_op | source)
XLA Modules:
  0.0 124.4 jit_solution(16674095146066111898)
XLA Ops:
  0.0 1.4 %copy.13 = bf16[1,128,8]{2,1,0:T(8,128)(2,1)} copy(bf16[1,128,8]{1,2,0:T(8,128)(2,1)} %param.18) | data formatting | bytes 4096 | tf_op args[7]
  1.4 1.4 %copy.12 = s32[1,128,8]{2,1,0:T(8,128)} copy(s32[1,128,8]{1,2,0:T(8,128)} %param.17) | data formatting | bytes 8192 | tf_op args[6]
  2.8 119.7 %layer.1 = bf16[128,2048]{1,0:T(8,128)(2,1)} custom-call(bf16[128,2048]{1,0:T(8,128)(2,1)} %bitcast.14, bf16[128,256]{1,0:T(8,128)(2,1)} %bitcast.18, bf16[128,256]{1,0:T(8,128)(2,1)} %bitcast.19, bf16[128,2048]{1,0:T(8,128)(2,1)} %bitcast.15, bf16[512,2048]{1,0:T(8,128)(2,1)} %proj_hbm.1, bf16[2048]{0:T(1024)(128)(2,1)} %gain_ref.1, s32[128,8]{1,0:T(8,128)} %bitcast.16, ...), custom_call_target="tpu_custom_call" | custom-call | tf_op jit(solution)/shard_map/layer/pallas_call | solution.py:806
  122.5 1.9 %copy.15 = bf16[1,128,2048]{2,1,0:T(8,128)(2,1)} copy(bf16[1,128,2048]{2,1,0:T(8,128)(2,1)} %bitcast.13) | data formatting | bytes 1048576

commit v3 on v2

--- a/solution.py
+++ b/solution.py
@@ -1,4 +1,5 @@
 import functools
+import math
 import jax
 import jax.numpy as jnp
 from jax import lax
@@ -177,28 +178,28 @@
 
 PLAN = [
     [
-        ("C", 0, 0), ("T", 1, 0), ("Y", 0, 0), ("T", 1, 1), ("Y", 0, 1), ("R", 0, 0),
-        ("C", 1, 0), ("C", 0, 1), ("T", 2, 0), ("Y", 1, 0), ("A", 1, 0), ("A", 1, 2),
-        ("T", 2, 1), ("C", 2, 0), ("Y", 2, 0), ("T", 3, 0), ("A", 2, 0), ("Y", 2, 1),
-        ("A", 2, 1), ("C", 2, 1), ("T", 3, 1), ("A", 2, 2), ("C", 3, 0), ("Y", 3, 0),
-        ("M", 2, 0), ("Y", 1, 1), ("S", 2, 3), ("C", 1, 1), ("Y", 3, 1), ("M", 2, 1),
-        ("S", 0, 0), ("C", 3, 1), ("M", 2, 2), ("S", 1, 1), ("A", 2, 3), ("S", 3, 0),
-        ("M", 1, 0), ("S", 3, 1), ("A", 3, 0), ("S", 3, 2), ("A", 3, 1), ("S", 3, 3),
-        ("A", 3, 2), ("S", 1, 3), ("A", 3, 3), ("S", 0, 1), ("M", 1, 2), ("S", 0, 2),
-        ("A", 0, 0), ("A", 1, 1), ("S", 0, 3), ("A", 0, 1), ("A", 1, 3), ("A", 0, 2),
+        ("C", 0, 0), ("T", 1, 0), ("Y", 0, 0), ("T", 1, 1), ("C", 1, 0), ("Y", 0, 1),
+        ("R", 0, 0), ("C", 0, 1), ("T", 2, 0), ("A", 1, 2), ("Y", 1, 0), ("A", 1, 3),
+        ("T", 2, 1), ("C", 2, 0), ("Y", 2, 0), ("T", 3, 0), ("A", 2, 0), ("A", 2, 1),
+        ("Y", 2, 1), ("A", 2, 2), ("C", 2, 1), ("T", 3, 1), ("A", 2, 3), ("C", 3, 0),
+        ("Y", 3, 0), ("Y", 1, 1), ("M", 2, 0), ("C", 1, 1), ("Y", 3, 1), ("M", 2, 1),
+        ("S", 0, 0), ("C", 3, 1), ("M", 2, 2), ("S", 1, 0), ("M", 2, 3), ("S", 3, 0),
+        ("M", 1, 2), ("S", 3, 1), ("A", 3, 0), ("S", 3, 2), ("A", 3, 1), ("S", 3, 3),
+        ("A", 3, 2), ("S", 1, 1), ("A", 3, 3), ("S", 0, 1), ("M", 1, 3), ("S", 0, 2),
+        ("A", 0, 0), ("A", 1, 0), ("S", 0, 3), ("A", 0, 1), ("A", 1, 1), ("A", 0, 2),
         ("A", 0, 3),
     ],
     [
         ("C", 1, 0), ("T", 0, 0), ("T", 2, 0), ("Y", 1, 0), ("T", 0, 1), ("T", 2, 1),
-        ("Y", 1, 1), ("C", 0, 0), ("C", 1, 1), ("T", 3, 0), ("Y", 0, 0), ("Y", 0, 1),
-        ("C", 2, 0), ("C", 0, 1), ("T", 3, 1), ("Y", 2, 0), ("R", 0, 0), ("C", 3, 0),
-        ("Y", 2, 1), ("C", 2, 1), ("M", 2, 3), ("Y", 3, 0), ("A", 2, 1), ("M", 0, 2),
-        ("S", 0, 0), ("A", 2, 2), ("Y", 3, 1), ("S", 0, 1), ("C", 3, 1), ("S", 2, 0),
-        ("M", 3, 3), ("S", 3, 0), ("M", 2, 1), ("S", 3, 1), ("A", 2, 0), ("S", 3, 2),
-        ("M", 2, 2), ("S", 0, 3), ("A", 2, 3), ("S", 1, 0), ("A", 3, 0), ("S", 1, 1),
-        ("A", 1, 0), ("A", 3, 1), ("S", 1, 3), ("A", 0, 0), ("A", 3, 2), ("A", 0, 1),
-        ("A", 3, 3), ("A", 0, 2), ("S", 1, 2), ("A", 0, 3), ("A", 1, 1), ("A", 1, 2),
-        ("A", 1, 3),
+        ("C", 0, 0), ("C", 2, 0), ("T", 3, 0), ("Y", 1, 1), ("C", 1, 1), ("Y", 0, 0),
+        ("Y", 0, 1), ("T", 3, 1), ("R", 0, 0), ("C", 0, 1), ("C", 3, 0), ("Y", 2, 0),
+        ("Y", 2, 1), ("A", 2, 0), ("C", 2, 1), ("M", 0, 0), ("Y", 3, 0), ("A", 2, 2),
+        ("M", 0, 1), ("A", 2, 3), ("S", 1, 1), ("M", 0, 3), ("Y", 3, 1), ("M", 2, 0),
+        ("C", 3, 1), ("S", 2, 1), ("M", 3, 2), ("S", 3, 0), ("M", 2, 2), ("S", 3, 1),
+        ("M", 0, 2), ("A", 2, 1), ("S", 3, 3), ("M", 2, 3), ("S", 1, 0), ("A", 3, 0),
+        ("S", 1, 2), ("A", 3, 1), ("A", 0, 0), ("A", 3, 2), ("A", 1, 2), ("A", 0, 1),
+        ("A", 3, 3), ("A", 0, 2), ("S", 1, 3), ("A", 0, 3), ("A", 1, 0), ("A", 1, 3),
+        ("A", 1, 1),
     ],
 ]
 CODES = "TYRCSMA"
@@ -248,13 +249,18 @@
     v_hbm,
     residual_hbm,
     proj_hbm,
+    gain_hbm,
+    ids_hbm,
+    gates_hbm,
+    wg_hbm,
+    wu_hbm,
+    wd_hbm,
+    o_hbm,
     gain_ref,
     ids_ref,
     gates_ref,
-    wg_hbm,
-    wu_hbm,
-    wd_hbm,
     o_ref,
+    o_sem,
     q_all,
     k_all,
     v_all,
@@ -351,14 +357,17 @@
         else:
             pl.when(condition)(action)
 
-    def query_part(s):
-        return q_hbm.at[:, pl.ds(pl.multiple_of(s * share, share), share)]
+    def query_part(s, h):
+        return q_hbm.at[pl.ds(h * half, half), pl.ds(pl.multiple_of(s * share, share), share)]
 
     def cache_part(ref, s):
         return ref.at[:, pl.ds(pl.multiple_of(s * heads // group * HD, HD), HD)]
 
     def token_rows(ref, s):
         return ref.at[pl.ds(pl.multiple_of(s * tokens, tokens), tokens), :]
+
+    def half_rows(s, h):
+        return pl.ds(pl.multiple_of(((s // 2 * 2 + h) * 2 + s % 2) * half, half), half)
 
     barrier = pltpu.get_barrier_semaphore()
     for peer in (across, partner, diagonal):
@@ -372,44 +381,39 @@
     def _():
         pl.semaphore_signal(barrier, 1, device_id=low, device_id_type=pl.DeviceIdType.MESH)
 
+    small = [
+        pltpu.make_async_copy(ids_hbm, ids_ref, load_sem.at[8]),
+        pltpu.make_async_copy(gates_hbm, gates_ref, load_sem.at[9]),
+    ]
     own_parts = [
-        pltpu.make_async_copy(query_part(seq), token_rows(q_all, seq), load_sem.at[0]),
         pltpu.make_async_copy(cache_part(k_hbm, seq), token_rows(k_all, seq), load_sem.at[1]),
         pltpu.make_async_copy(cache_part(v_hbm, seq), token_rows(v_all, seq), load_sem.at[2]),
+        pltpu.make_async_copy(query_part(seq, 0), q_all.at[half_rows(seq, 0), :], load_sem.at[0]),
+        pltpu.make_async_copy(query_part(seq, 1), q_all.at[half_rows(seq, 1), :], load_sem.at[11]),
         pltpu.make_async_copy(proj_hbm, proj, load_sem.at[3]),
     ]
     loads = [
         pltpu.make_async_copy(residual_hbm, residual, load_sem.at[7]),
+        pltpu.make_async_copy(gain_hbm, gain_ref, load_sem.at[10]),
         pltpu.make_async_copy(wg_hbm, wg, load_sem.at[4]),
         pltpu.make_async_copy(wu_hbm, wu, load_sem.at[5]),
         pltpu.make_async_copy(wd_hbm, wd, load_sem.at[6]),
     ]
-    for load in own_parts + loads:
+    for load in small + own_parts + loads:
         load.start()
 
-    lanes = 128 * ((4 * n_sub + 127) // 128)
-    lane = lax.broadcasted_iota(jnp.int32, (tokens, lanes), 1)
+    def coef_tile(p, s, count=1):
+        return pl.ds(pl.multiple_of((p * 4 + s) * tile, tile), count * tile)
+
+    for load in small:
+        load.wait()
+    expert = lax.broadcasted_iota(jnp.int32, (tile, tokens), 0)
     ids = ids_ref[...]
     gates = gates_ref[...].astype(jnp.float32)
-    weights_here = jnp.zeros((tokens, lanes), jnp.float32)
-    for k in range(ids.shape[1]):
-        weights_here = weights_here + jnp.where(ids[:, k : k + 1] == lane, gates[:, k : k + 1], 0.0)
-    identity = (
-        lax.broadcasted_iota(jnp.int32, (tokens, tokens), 0)
-        == lax.broadcasted_iota(jnp.int32, (tokens, tokens), 1)
-    ).astype(jnp.float32).astype(jnp.bfloat16)
-    turned = lax.dot_general(
-        weights_here.astype(jnp.bfloat16),
-        identity,
-        (((0,), (0,)), ((), ())),
-        preferred_element_type=jnp.float32,
-    )
-
-    def coef_tile(p, s, count=1):
-        return pl.ds(pl.multiple_of((p * 4 + s) * tile, tile), count * tile)
-
-    coef[coef_tile(z, seq), :] = turned[:tile].astype(jnp.bfloat16)
-
+    weights_here = jnp.zeros((tile, tokens), jnp.float32)
+    for k in range(ids.shape[0]):
+        weights_here = weights_here + jnp.where(ids[k : k + 1, :] == expert, gates[k : k + 1, :], 0.0)
+    coef[coef_tile(z, seq), :] = weights_here.astype(jnp.bfloat16)
     peers = 3 + jnp.where(has_high, 1, 0) + jnp.where(has_low, 1, 0)
     with jax.named_scope("BAR"):
         pl.semaphore_wait(barrier, peers)
@@ -420,7 +424,7 @@
         (y * 2 + 1 - c, partner),
     )
 
-    def scatter_copies(s, target):
+    def cache_copies(s, target):
         return (
             remote(
                 cache_part(k_hbm, s),
@@ -436,9 +440,15 @@
                 kv_recv.at[4 + seq],
                 target,
             ),
-            remote(
-                query_part(s), token_rows(q_all, seq), q_send.at[s], q_recv.at[seq], target
-            ),
+        )
+
+    def query_copy(s, h, target):
+        return remote(
+            query_part(s, h),
+            q_all.at[half_rows(seq, h), :],
+            q_send.at[s * 2 + h],
+            q_recv.at[seq * 2 + h],
+            target,
         )
 
     def coef_near(s, target):
@@ -447,9 +457,11 @@
 
     for s, target in others:
         coef_near(s, target).start()
-    for s, target in others:
-        for copy in scatter_copies(s, target):
+        for copy in cache_copies(s, target):
             copy.start()
+    for h in range(2):
+        for s, target in others:
+            query_copy(s, h, target).start()
 
     def arrival(ref, s, sem):
         return remote(token_rows(ref, s), token_rows(ref, s), q_send.at[s], sem, partner)
@@ -475,100 +487,124 @@
         for s, _ in others:
             arrival(k_all, s, kv_recv.at[s]).wait_recv()
             arrival(v_all, s, kv_recv.at[4 + s]).wait_recv()
-            arrival(q_all, s, q_recv.at[s]).wait_recv()
-
-    for s, target in others:
-        there = coef.at[coef_tile(z, s), :]
-        remote(there, there, coef_send.at[s], coef_recv.at[s], target).wait_recv()
-    pl.when(has_high)(lambda: coef_hop(z, coef_up, high).start())
-    pl.when(has_low)(lambda: coef_hop(z, coef_down, low).start())
-
-    far_copy = remote(
-        token_rows(partial, (1 - y) * 2 + 1 - c), core_far, part_send.at[0], part_recv.at[0], partner
-    )
-    across_copy = remote(
-        token_rows(partial, (1 - y) * 2 + c),
-        across_near,
-        part_send.at[1],
-        part_recv.at[1],
-        across,
-    )
-    near_copy = remote(
-        token_rows(partial, y * 2 + 1 - c), core_near, part_send.at[2], part_recv.at[2], partner
-    )
-
-    def attend_step(j, carry):
-        yy = jnp.where(j < 2, 1 - y, y)
-        cc = jnp.where(j % 2 == 0, 1 - c, c)
-        i = yy * 2 + cc
-        at = pl.ds(pl.multiple_of(i * tokens, tokens), tokens)
-        row_pos = i * tokens + lax.broadcasted_iota(jnp.int32, (tokens, length), 0)
-        col_pos = lax.broadcasted_iota(jnp.int32, (tokens, length), 1)
-        allowed = row_pos >= col_pos
-        outputs = []
-        for head in range(heads):
+
+    def half_copy(src_rows, dst, h, at, target):
+        return remote(
+            partial.at[src_rows, :],
+            dst.at[pl.ds(pl.multiple_of(h * half, half), half), :],
+            part_send.at[at * 2 + h],
+            part_recv.at[at * 2 + h],
+            target,
+        )
+
+    def far_copy(h):
+        return half_copy(half_rows((1 - y) * 2 + 1 - c, h), core_far, h, 0, partner)
+
+    def across_copy(h):
+        return half_copy(half_rows((1 - y) * 2 + c, h), across_near, h, 1, across)
+
+    def near_copy(h):
+        return half_copy(half_rows(y * 2 + 1 - c, h), core_near, h, 2, partner)
+
+    def half_at(h):
+        return pl.ds(pl.multiple_of(h * half, half), half)
+
+    def attend_step(t, carry):
+        h = t // 2
+        other = jnp.logical_or(t == 1, t == 2)
+        yy = jnp.where(other, 1 - y, y)
+        at = pl.ds(pl.multiple_of((yy * 2 + h) * tokens, tokens), tokens)
+
+        for cc in range(2):
+
+            @pl.when(yy * 2 + cc != seq)
+            def _():
+                block = q_all.at[half_rows(yy * 2 + cc, h), :]
+                arrived = q_recv.at[(yy * 2 + cc) * 2 + h]
+                remote(block, block, q_send.at[0], arrived, partner).wait_recv()
+
+        @pl.when(t == 2)
+        def _():
+            send_sum(0)
+
+        with jax.named_scope("A1"):
+            row = lax.broadcasted_iota(jnp.int32, (tokens, 1), 0)
+            row_pos = yy * 2 * tokens + h * half + row + jnp.where(row >= half, tokens - half, 0)
+            col_pos = lax.broadcasted_iota(jnp.int32, (tokens, length), 1)
+            allowed = row_pos >= col_pos
             scores = lax.dot_general(
-                q_all[at, head * HD : (head + 1) * HD],
+                jnp.concatenate([q_all[at, head * HD : (head + 1) * HD] for head in range(heads)], axis=0),
                 k_all[...],
                 (((1,), (1,)), ((), ())),
                 preferred_element_type=jnp.float32,
-            ) * (1.0 / HD**0.5)
-            scores = jnp.where(allowed, scores, -1e30)
-            weights = jnp.exp(scores - jnp.max(scores, axis=1, keepdims=True))
-            total = jnp.sum(weights, axis=1, keepdims=True)
-            probs = (weights * (1.0 / total)).astype(jnp.bfloat16)
-            outputs.append(
-                jnp.dot(probs, v_all[...], preferred_element_type=jnp.float32).astype(jnp.bfloat16)
             )
-        projected = jnp.dot(
+            chances, totals = [], []
+            for head in range(heads):
+                raw = jnp.where(allowed, scores[head * tokens : (head + 1) * tokens], -1e30)
+                peak = jnp.max(raw, axis=1, keepdims=True)
+                weights = jnp.exp2((raw - peak) * (math.log2(math.e) / HD**0.5))
+                totals.append(jnp.sum(weights, axis=1, keepdims=True))
+                chances.append(weights.astype(jnp.bfloat16))
+            mixed = jnp.dot(
+                jnp.concatenate(chances, axis=0), v_all[...], preferred_element_type=jnp.float32
+            )
+            outputs = [
+                (mixed[head * tokens : (head + 1) * tokens] * (1.0 / totals[head])).astype(jnp.bfloat16)
+                for head in range(heads)
+            ]
+        partial[at, :] = jnp.dot(
             jnp.concatenate(outputs, axis=1), proj[...], preferred_element_type=jnp.float32
-        )
-
-        @pl.when(j != 1)
-        def _():
-            partial[at, :] = projected.astype(jnp.bfloat16)
-
-        @pl.when(j == 0)
-        def _():
-            far_copy.start()
-
-        @pl.when(j == 1)
-        def _():
-            far_copy.wait_recv()
-            partial[at, :] = (projected + core_far[...].astype(jnp.float32)).astype(jnp.bfloat16)
-            across_copy.start()
-
-        @pl.when(j == 2)
-        def _():
-            near_copy.start()
-
+        ).astype(jnp.bfloat16)
+
+        pl.when(other)(lambda: far_copy(h).start())
+        pl.when(jnp.logical_not(other))(lambda: near_copy(h).start())
+
+        @pl.when(t == 0)
+        def _():
+            for s, target in others:
+                there = coef.at[coef_tile(z, s), :]
+                remote(there, there, coef_send.at[s], coef_recv.at[s], target).wait_recv()
+            pl.when(has_high)(lambda: coef_hop(z, coef_up, high).start())
+            pl.when(has_low)(lambda: coef_hop(z, coef_down, low).start())
+
+        pl.when(t == 1)(lambda: coef_step(1))
         return carry
+
+    def send_sum(h):
+        far_copy(h).wait_recv()
+        at = half_rows((1 - y) * 2 + c, h)
+        total = partial[at, :].astype(jnp.float32) + core_far[half_at(h), :].astype(jnp.float32)
+        partial[at, :] = total.astype(jnp.bfloat16)
+        across_copy(h).start()
 
     with jax.named_scope("ATT"):
         lax.fori_loop(0, 4, attend_step, 0)
-    coef_step(1)
+    send_sum(1)
+    coef_step(2)
     for load in loads:
         load.wait()
-    coef_step(2)
-    near_copy.wait_recv()
-    own_rows = pl.ds(pl.multiple_of(seq * tokens, tokens), tokens)
-    base = (
-        residual[...].astype(jnp.float32)
-        + partial[own_rows, :].astype(jnp.float32)
-        + core_near[...].astype(jnp.float32)
-    )
-    with jax.named_scope("ACR"):
-        across_copy.wait_recv()
-    hidden = (base + across_near[...].astype(jnp.float32)).astype(jnp.bfloat16)
-    wide_ref[...] = hidden
-    wide = hidden.astype(jnp.float32)
-    normed = (
-        wide
-        * lax.rsqrt(jnp.mean(wide * wide, axis=1, keepdims=True) + 1e-06)
-        * gain_ref[...].astype(jnp.float32)[None, :]
-    ).astype(jnp.bfloat16)
-    own_slot = pl.ds(pl.multiple_of(slot(y, z, c) * tokens, tokens), tokens)
-    rows[own_slot, :] = normed
+
+    def finish(h):
+        near_copy(h).wait_recv()
+        with jax.named_scope("ACR"):
+            across_copy(h).wait_recv()
+        at = half_at(h)
+        hidden = (
+            residual[at, :].astype(jnp.float32)
+            + partial[half_rows(seq, h), :].astype(jnp.float32)
+            + core_near[at, :].astype(jnp.float32)
+            + across_near[at, :].astype(jnp.float32)
+        ).astype(jnp.bfloat16)
+        wide_ref[at, :] = hidden
+        wide = hidden.astype(jnp.float32)
+        normed = (
+            wide
+            * lax.rsqrt(jnp.mean(wide * wide, axis=1, keepdims=True) + 1e-06)
+            * gain_ref[...].astype(jnp.float32)[None, :]
+        ).astype(jnp.bfloat16)
+        index = slot(y, z, c)
+        rows[pl.ds(pl.multiple_of(index * tokens + h * half, half), half), :] = normed
+        spread(z, h)
 
     def row_copy(index, h, send, target):
         here = piece(rows, index, h)
@@ -634,8 +670,8 @@
     def mate_rows():
         return row_copy(slot(1 - y, z, c), 1, mate_send.at[0], beside)
 
-    spread(z, 0)
-    spread(z, 1)
+    finish(0)
+    finish(1)
     coef_step(3)
 
     def part(index, q):
@@ -671,6 +707,9 @@
         here = part(index, q)
         total = outs[here, :].astype(jnp.float32) + ref[part(at, q_at), :].astype(jnp.float32)
         outs[here, :] = total.astype(jnp.bfloat16)
+
+    def out_copy(q):
+        return pltpu.make_async_copy(o_ref.at[part(0, q), :], o_hbm.at[part(0, q), :], o_sem.at[q])
 
     def toward(p):
         return jnp.where(p > z, 0, 1)
@@ -748,6 +787,7 @@
                 o_ref[at, :] = (
                     wide_ref[at, :].astype(jnp.float32) + outs[part(index, q), :].astype(jnp.float32)
                 ).astype(jnp.bfloat16)
+                out_copy(q).start()
 
         return carry
 
@@ -785,13 +825,18 @@
                     line_copy(p, q, toward(p)).wait_send()
 
     for s, target in others:
-        for copy in scatter_copies(s, target):
+        for copy in cache_copies(s, target):
             copy.wait_send()
         coef_near(s, target).wait_send()
+        for h in range(2):
+            query_copy(s, h, target).wait_send()
     mate_rows().wait_send()
-    far_copy.wait_send()
-    across_copy.wait_send()
-    near_copy.wait_send()
+    for h in range(2):
+        far_copy(h).wait_send()
+        across_copy(h).wait_send()
+        near_copy(h).wait_send()
+    for q in range(4):
+        out_copy(q).wait()
 
 
 def layer(queries, keys, values, residual, proj, gain, ids, gates, w_gate, w_up, w_down, n_sub):
@@ -801,14 +846,18 @@
     tile = 16 * ((blocks + 15) // 16)
     dma = lambda count: pltpu.SemaphoreType.DMA((count,))
     hbm = pl.BlockSpec(memory_space=pl.ANY)
-    vmem = pl.BlockSpec(memory_space=pltpu.VMEM)
     bf = jnp.bfloat16
     return pl.pallas_call(
         functools.partial(layer_kernel, n_sub),
-        in_specs=[hbm, hbm, hbm, hbm, hbm, vmem, vmem, vmem, hbm, hbm, hbm],
-        out_specs=vmem,
+        in_specs=[hbm] * 11,
+        out_specs=hbm,
         out_shape=jax.ShapeDtypeStruct((tokens, width), bf),
         scratch_shapes=[
+            pltpu.VMEM(gain.shape, bf),
+            pltpu.VMEM(ids.shape, jnp.int32),
+            pltpu.VMEM(gates.shape, bf),
+            pltpu.VMEM((tokens, width), bf),
+            dma(4),
             pltpu.VMEM((4 * tokens, share), bf),
             pltpu.VMEM((4 * tokens, HD), bf),
             pltpu.VMEM((4 * tokens, HD), bf),
@@ -819,12 +868,12 @@
             pltpu.VMEM((tokens, width), bf),
             pltpu.VMEM((tokens, width), bf),
             pltpu.VMEM((tokens, width), bf),
-            dma(4),
-            dma(4),
             dma(8),
             dma(8),
-            dma(3),
-            dma(3),
+            dma(8),
+            dma(8),
+            dma(6),
+            dma(6),
             pltpu.VMEM((blocks * tile, tokens), bf),
             dma(4),
             dma(4),
@@ -840,7 +889,7 @@
             pltpu.VMEM(w_gate.shape, bf),
             pltpu.VMEM(w_up.shape, bf),
             pltpu.VMEM(w_down.shape, bf),
-            dma(8),
+            dma(12),
             dma(2 * blocks),
             dma(2 * n_sub),
             dma(2 * n_sub),
@@ -884,8 +933,8 @@
         residual_in[0],
         out_proj,
         norm_gain,
-        expert_ids[0],
-        gate_weights[0],
+        expert_ids[0].T,
+        gate_weights[0].T,
         expert_gate[0],
         expert_up[0],
         expert_down[0],

time: 125 us -> 113 us (0.904)
  Pallas kernels: 120 us -> 111 us
  local copies, waits for them, and re-layouts: 4.68 us -> 1.88 us
    pallas_call x1, Pallas kernels: 120 us -> 111 us  [layer(): pl.pallas_call(functools.partial(layer_kernel, n_sub), in_specs=[hbm] * 1...]
    unnamed x3 -> x1, local copies, waits for them, and re-layouts: 4.68 us -> 1.88 us
where the time goes in v3:
time: 113 us; the launch traced here: 112 us
  Pallas kernels  111 us (98%)
  local copies, waits for them, and re-layouts  1.88 us (2%)
    pallas_call x1, Pallas kernels, layer(): pl.pallas_call(functools.partial(layer_kernel, n_sub), in_specs=[hbm] * 1...  111 us

profile of v3, /device:TPU:0, one launch (start us, length us, event | category | flops | bytes accessed | tf_op | source)
XLA Modules:
  0.0 112.4 jit_solution(8835048024702005913)
XLA Ops:
  0.0 110.5 %layer.1 = bf16[128,2048]{1,0:T(8,128)(2,1)} custom-call(bf16[128,2048]{1,0:T(8,128)(2,1)} %bitcast.18, bf16[128,256]{1,0:T(8,128)(2,1)} %bitcast.20, bf16[128,256]{1,0:T(8,128)(2,1)} %bitcast.21, bf16[128,2048]{1,0:T(8,128)(2,1)} %bitcast.19, bf16[512,2048]{1,0:T(8,128)(2,1)} %proj_hbm.1, bf16[2048]{0:T(1024)(128)(2,1)} %gain_hbm.1, s32[8,128]{1,0:T(8,128)} %bitcast.22, ...), custom_call_target="tpu_custom_call" | custom-call | tf_op jit(solution)/shard_map/layer/pallas_call | solution.py:850
  110.6 1.9 %copy.13 = bf16[1,128,2048]{2,1,0:T(8,128)(2,1)} copy(bf16[1,128,2048]{2,1,0:T(8,128)(2,1)} %bitcast.17) | data formatting | bytes 1048576

commit v4 on v3

--- a/solution.py
+++ b/solution.py
@@ -178,28 +178,30 @@
 
 PLAN = [
     [
-        ("C", 0, 0), ("T", 1, 0), ("Y", 0, 0), ("T", 1, 1), ("C", 1, 0), ("Y", 0, 1),
-        ("R", 0, 0), ("C", 0, 1), ("T", 2, 0), ("A", 1, 2), ("Y", 1, 0), ("A", 1, 3),
-        ("T", 2, 1), ("C", 2, 0), ("Y", 2, 0), ("T", 3, 0), ("A", 2, 0), ("A", 2, 1),
-        ("Y", 2, 1), ("A", 2, 2), ("C", 2, 1), ("T", 3, 1), ("A", 2, 3), ("C", 3, 0),
-        ("Y", 3, 0), ("Y", 1, 1), ("M", 2, 0), ("C", 1, 1), ("Y", 3, 1), ("M", 2, 1),
-        ("S", 0, 0), ("C", 3, 1), ("M", 2, 2), ("S", 1, 0), ("M", 2, 3), ("S", 3, 0),
-        ("M", 1, 2), ("S", 3, 1), ("A", 3, 0), ("S", 3, 2), ("A", 3, 1), ("S", 3, 3),
-        ("A", 3, 2), ("S", 1, 1), ("A", 3, 3), ("S", 0, 1), ("M", 1, 3), ("S", 0, 2),
-        ("A", 0, 0), ("A", 1, 0), ("S", 0, 3), ("A", 0, 1), ("A", 1, 1), ("A", 0, 2),
-        ("A", 0, 3),
+        ("C", 0, 2), ("T", 1, 0), ("C", 1, 0), ("Y", 0, 0), ("C", 0, 1), ("T", 1, 1),
+        ("C", 1, 2), ("Y", 0, 1), ("R", 0, 0), ("C", 0, 3), ("T", 2, 0), ("A", 1, 0),
+        ("C", 2, 0), ("Y", 1, 0), ("A", 1, 1), ("C", 1, 1), ("T", 2, 1), ("A", 2, 0),
+        ("C", 2, 2), ("Y", 2, 0), ("M", 1, 0), ("C", 2, 1), ("T", 3, 0), ("M", 1, 1),
+        ("C", 3, 0), ("Y", 2, 1), ("M", 2, 0), ("C", 2, 3), ("T", 3, 1), ("A", 3, 0),
+        ("C", 3, 2), ("Y", 3, 0), ("M", 2, 3), ("C", 3, 1), ("Y", 1, 1), ("S", 2, 1),
+        ("A", 2, 3), ("C", 1, 3), ("Y", 3, 1), ("S", 3, 1), ("M", 3, 0), ("C", 3, 3),
+        ("S", 2, 2), ("M", 1, 2), ("S", 3, 2), ("A", 3, 1), ("S", 3, 3), ("A", 2, 1),
+        ("S", 1, 3), ("A", 3, 2), ("S", 0, 1), ("A", 3, 3), ("S", 0, 0), ("A", 2, 2),
+        ("S", 0, 2), ("A", 1, 2), ("A", 0, 1), ("S", 0, 3), ("A", 0, 0), ("A", 1, 3),
+        ("A", 0, 2), ("A", 0, 3),
     ],
     [
-        ("C", 1, 0), ("T", 0, 0), ("T", 2, 0), ("Y", 1, 0), ("T", 0, 1), ("T", 2, 1),
-        ("C", 0, 0), ("C", 2, 0), ("T", 3, 0), ("Y", 1, 1), ("C", 1, 1), ("Y", 0, 0),
-        ("Y", 0, 1), ("T", 3, 1), ("R", 0, 0), ("C", 0, 1), ("C", 3, 0), ("Y", 2, 0),
-        ("Y", 2, 1), ("A", 2, 0), ("C", 2, 1), ("M", 0, 0), ("Y", 3, 0), ("A", 2, 2),
-        ("M", 0, 1), ("A", 2, 3), ("S", 1, 1), ("M", 0, 3), ("Y", 3, 1), ("M", 2, 0),
-        ("C", 3, 1), ("S", 2, 1), ("M", 3, 2), ("S", 3, 0), ("M", 2, 2), ("S", 3, 1),
-        ("M", 0, 2), ("A", 2, 1), ("S", 3, 3), ("M", 2, 3), ("S", 1, 0), ("A", 3, 0),
-        ("S", 1, 2), ("A", 3, 1), ("A", 0, 0), ("A", 3, 2), ("A", 1, 2), ("A", 0, 1),
-        ("A", 3, 3), ("A", 0, 2), ("S", 1, 3), ("A", 0, 3), ("A", 1, 0), ("A", 1, 3),
-        ("A", 1, 1),
+        ("C", 1, 2), ("T", 0, 0), ("T", 2, 0), ("C", 0, 0), ("Y", 1, 0), ("C", 2, 0),
+        ("T", 0, 1), ("T", 2, 1), ("C", 1, 1), ("C", 0, 2), ("C", 2, 2), ("Y", 1, 1),
+        ("T", 3, 0), ("C", 1, 3), ("C", 3, 0), ("Y", 0, 0), ("Y", 0, 1), ("C", 0, 1),
+        ("T", 3, 1), ("R", 0, 0), ("C", 0, 3), ("C", 3, 2), ("Y", 2, 0), ("C", 2, 1),
+        ("A", 2, 0), ("M", 2, 1), ("Y", 2, 1), ("C", 2, 3), ("M", 0, 3), ("M", 2, 2),
+        ("Y", 3, 0), ("M", 2, 0), ("C", 3, 1), ("S", 1, 1), ("A", 3, 0), ("M", 3, 1),
+        ("S", 1, 3), ("Y", 3, 1), ("C", 3, 3), ("S", 2, 3), ("A", 0, 0), ("M", 3, 2),
+        ("S", 3, 3), ("M", 0, 1), ("M", 3, 0), ("S", 1, 0), ("A", 2, 3), ("S", 0, 2),
+        ("M", 0, 0), ("A", 3, 1), ("S", 1, 2), ("A", 1, 0), ("A", 2, 1), ("A", 0, 1),
+        ("A", 3, 2), ("A", 1, 1), ("A", 3, 3), ("A", 0, 2), ("A", 2, 2), ("A", 0, 3),
+        ("A", 1, 2), ("A", 1, 3),
     ],
 ]
 CODES = "TYRCSMA"
@@ -214,7 +216,7 @@
         for what, p, q in steps:
             first = one = two = 0
             if what in "SMA":
-                key = (what == "A", p)
+                key = (what == "A", p, q // 2)
                 first = int(key not in met)
                 met.add(key)
             if what == "A":
@@ -338,8 +340,11 @@
     def slot(yy, p, cc):
         return (yy * n_sub + p) * 2 + cc
 
+    def piece_start(index, h):
+        return ((index // 2 * 2 + h) * 2 + index % 2) * half
+
     def piece(ref, index, h):
-        return ref.at[pl.ds(pl.multiple_of(index * tokens + h * half, half), half), :]
+        return ref.at[pl.ds(pl.multiple_of(piece_start(index, h), half), half), :]
 
     def remote(src, dst, send, recv, target):
         return pltpu.make_async_remote_copy(
@@ -581,7 +586,7 @@
         lax.fori_loop(0, 4, attend_step, 0)
     send_sum(1)
     coef_step(2)
-    for load in loads:
+    for load in loads[:2]:
         load.wait()
 
     def finish(h):
@@ -603,7 +608,7 @@
             * gain_ref[...].astype(jnp.float32)[None, :]
         ).astype(jnp.bfloat16)
         index = slot(y, z, c)
-        rows[pl.ds(pl.multiple_of(index * tokens + h * half, half), half), :] = normed
+        rows[pl.ds(pl.multiple_of(piece_start(index, h), half), half), :] = normed
         spread(z, h)
 
     def row_copy(index, h, send, target):
@@ -633,54 +638,61 @@
     def relay_copy(p, h):
         return row_copy(slot(1 - y, p, c), h, relay_send.at[p * 2 + h], partner)
 
-    def result_copy(yy, p):
-        index = slot(yy, p, 1 - c)
+    def result_copy(yy, p, h):
         pair = yy * n_sub + p
-        src = outs.at[pl.ds(pl.multiple_of(index * tokens, tokens), tokens), :]
-        dst = from_core.at[pl.ds(pl.multiple_of(pair * tokens, tokens), tokens), :]
-        return remote(src, dst, result_send.at[pair], core_recv.at[pair], partner)
+        dst = from_core.at[pl.ds(pl.multiple_of(pair * tokens + h * half, half), half), :]
+        at = pair * 2 + h
+        return remote(
+            piece(outs, slot(yy, p, 1 - c), h), dst, result_send.at[at], core_recv.at[at], partner
+        )
 
     mine = (
-        lax.broadcasted_iota(jnp.int32, (2 * tile, 128), 0) % tile == me
+        lax.broadcasted_iota(jnp.int32, (tile, 128), 0) == me
     ).astype(jnp.float32).astype(jnp.bfloat16)
 
-    def compute(yy, p):
-        wait_rows(slot(yy, p, 1 - c), 0)
-        wait_rows(slot(yy, p, 1 - c), 1)
+    def compute(yy, p, h):
+        wait_rows(slot(yy, p, 1 - c), h)
         with jax.named_scope("C"):
-            at = pl.ds(pl.multiple_of((yy * n_sub + p) * 2 * tokens, 2 * tokens), 2 * tokens)
+            at = pl.ds(pl.multiple_of(((yy * n_sub + p) * 2 + h) * tokens, tokens), tokens)
             x = rows[at, :]
-            gains = [
-                lax.dot_general(
+            gains = []
+            for cc in range(2):
+                both = lax.dot_general(
                     coef[coef_tile(p, 2 * yy + cc), :],
-                    mine[:tile],
+                    mine,
                     (((0,), (0,)), ((), ())),
                     preferred_element_type=jnp.float32,
                 )
-                for cc in range(2)
-            ]
+                gains.append(jnp.where(h == 0, both[:half], both[half:]))
             coeff = jnp.concatenate(gains, axis=0)[:, :1]
             gate = jnp.dot(x, wg[...], preferred_element_type=jnp.float32)
             up = jnp.dot(x, wu[...], preferred_element_type=jnp.float32)
             inner = (gate / (1.0 + jnp.exp(-gate)) * up).astype(jnp.bfloat16)
             out = jnp.dot(inner, wd[...], preferred_element_type=jnp.float32)
             outs[at, :] = (out * coeff).astype(jnp.bfloat16)
-        result_copy(yy, p).start()
+        result_copy(yy, p, h).start()
 
     def mate_rows():
         return row_copy(slot(1 - y, z, c), 1, mate_send.at[0], beside)
 
     finish(0)
+    for load in loads[2:]:
+        load.wait()
+    compute(y, z, 0)
     finish(1)
     coef_step(3)
 
     def part(index, q):
         return pl.ds(pl.multiple_of(index * tokens + q * quarter, quarter), quarter)
+
+    def sums(index, q):
+        start = piece_start(index, q // 2) + q % 2 * quarter
+        return pl.ds(pl.multiple_of(start, quarter), quarter)
 
     def y_copy(p, q):
         at = p * 4 + q
         return remote(
-            outs.at[part(slot(1 - y, p, c), q), :],
+            outs.at[sums(slot(1 - y, p, c), q), :],
             from_y.at[part(p, q), :],
             result_y_send.at[at],
             y_recv.at[at],
@@ -690,7 +702,7 @@
     def passed(yy, p, q, way, buffer, send, recv):
         at = p * 4 + q
         return remote(
-            outs.at[part(slot(yy, p, c), q), :],
+            outs.at[sums(slot(yy, p, c), q), :],
             buffer.at[part(way * n_sub + p, q), :],
             send.at[at],
             recv.at[way * 4 * n_sub + at],
@@ -704,7 +716,7 @@
         return passed(1 - y, p, q, way, from_moved, moved_send, moved_recv)
 
     def add_to(index, q, ref, at, q_at):
-        here = part(index, q)
+        here = sums(index, q)
         total = outs[here, :].astype(jnp.float32) + ref[part(at, q_at), :].astype(jnp.float32)
         outs[here, :] = total.astype(jnp.bfloat16)
 
@@ -740,12 +752,12 @@
 
         @pl.when(what == CODES.index("C"))
         def _():
-            compute(jnp.where(q == 1, 1 - y, y), p)
+            compute(jnp.where(q % 2 == 1, 1 - y, y), p, q // 2)
 
         @pl.when(jnp.logical_or(what == CODES.index("S"), what == CODES.index("M")))
         def _():
             index = slot(1 - y, p, c)
-            pl.when(first == 1)(lambda: result_copy(1 - y, p).wait_recv())
+            pl.when(first == 1)(lambda: result_copy(1 - y, p, q // 2).wait_recv())
             add_to(index, q, from_core, (1 - y) * n_sub + p, q)
 
             @pl.when(one == 1)
@@ -764,7 +776,7 @@
         @pl.when(what == CODES.index("A"))
         def _():
             index = slot(y, p, c)
-            pl.when(first == 1)(lambda: result_copy(y, p).wait_recv())
+            pl.when(first == 1)(lambda: result_copy(y, p, q // 2).wait_recv())
             add_to(index, q, from_core, y * n_sub + p, q)
 
             @pl.when(one == 1)
@@ -785,7 +797,7 @@
             def _():
                 at = part(0, q)
                 o_ref[at, :] = (
-                    wide_ref[at, :].astype(jnp.float32) + outs[part(index, q), :].astype(jnp.float32)
+                    wide_ref[at, :].astype(jnp.float32) + outs[sums(index, q), :].astype(jnp.float32)
                 ).astype(jnp.bfloat16)
                 out_copy(q).start()
 
@@ -801,7 +813,8 @@
             guarded(condition, copy.wait_send)
 
         relay_copy(p, h).wait_send()
-        result_copy(h, p).wait_send()
+        result_copy(0, p, h).wait_send()
+        result_copy(1, p, h).wait_send()
 
         @pl.when(h == 0)
         def _():
@@ -896,8 +909,8 @@
             dma(2 * n_sub),
             dma(2 * n_sub),
             dma(2 * n_sub),
-            dma(2 * n_sub),
-            dma(2 * n_sub),
+            dma(4 * n_sub),
+            dma(4 * n_sub),
             dma(4 * n_sub),
             dma(4 * n_sub),
             dma(8 * n_sub),

time: 113 us -> 109 us (0.965)
  Pallas kernels: 111 us -> 107 us
    pallas_call x1, Pallas kernels: 111 us -> 107 us  [layer(): pl.pallas_call(functools.partial(layer_kernel, n_sub), in_specs=[hbm] * 1...]
where the time goes in v4:
time: 109 us; the launch traced here: 108 us
  Pallas kernels  107 us (98%)
  local copies, waits for them, and re-layouts  1.88 us (2%)
    pallas_call x1, Pallas kernels, layer(): pl.pallas_call(functools.partial(layer_kernel, n_sub), in_specs=[hbm] * 1...  107 us

profile of v4, /device:TPU:0, one launch (start us, length us, event | category | flops | bytes accessed | tf_op | source)
XLA Modules:
  0.0 108.4 jit_solution(757444726049393122)
XLA Ops:
  0.0 106.5 %layer.1 = bf16[128,2048]{1,0:T(8,128)(2,1)} custom-call(bf16[128,2048]{1,0:T(8,128)(2,1)} %bitcast.18, bf16[128,256]{1,0:T(8,128)(2,1)} %bitcast.20, bf16[128,256]{1,0:T(8,128)(2,1)} %bitcast.21, bf16[128,2048]{1,0:T(8,128)(2,1)} %bitcast.19, bf16[512,2048]{1,0:T(8,128)(2,1)} %proj_hbm.1, bf16[2048]{0:T(1024)(128)(2,1)} %gain_hbm.1, s32[8,128]{1,0:T(8,128)} %bitcast.22, ...), custom_call_target="tpu_custom_call" | custom-call | tf_op jit(solution)/shard_map/layer/pallas_call | solution.py:863
  106.5 1.9 %copy.13 = bf16[1,128,2048]{2,1,0:T(8,128)(2,1)} copy(bf16[1,128,2048]{2,1,0:T(8,128)(2,1)} %bitcast.17) | data formatting | bytes 1048576
